TPU v7x, 32 devices: a whole 2x2x4 slice. The times are simulated.
32 devices in a mesh: ctx: 4 (over x, core), fsdp: 4 (over z), rep: 2 (over y).
Axes of the slice: x: 2, y: 2, z: 4, core: 2. Of those that a mesh axis runs over, the one named last changes fastest.
Arguments:
- tokens: bfloat16 [8, 1024, 1024], P(('fsdp', 'rep'), 'ctx'), may hold values from -6 to 6
- segments: int32 [8, 1024], P(('fsdp', 'rep')), may hold values from 0 to 4, never falling along the last dimension, each value on 1 to 800 neighbouring positions
- ln1_gain: bfloat16 [1024], P(('ctx', 'fsdp')), may hold values from 0.5 to 1.5
- ln1_bias: bfloat16 [1024], P(('ctx', 'fsdp')), may hold values from -1 to 1
- w_qkv: bfloat16 [1024, 3072], P(('ctx', 'fsdp')), may hold values from -0.1875 to 0.1875
- q_bias: bfloat16 [1024], P(('ctx', 'fsdp')), may hold values from -1.5 to 1.5
- v_bias: bfloat16 [1024], P(('ctx', 'fsdp')), may hold values from -1.5 to 1.5
- w_out: bfloat16 [1024, 1024], P(('ctx', 'fsdp')), may hold values from -0.5 to 0.5
- out_bias: bfloat16 [1024], P(('ctx', 'fsdp')), may hold values from -1.5 to 1.5
- ln2_gain: bfloat16 [1024], P(('ctx', 'fsdp')), may hold values from 0.5 to 1.5
- ln2_bias: bfloat16 [1024], P(('ctx', 'fsdp')), may hold values from -1 to 1
- w_in: bfloat16 [1024, 4096], P(('ctx', 'fsdp')), may hold values from -0.1875 to 0.1875
- in_bias: bfloat16 [4096], P(('ctx', 'fsdp')), may hold values from -1.5 to 1.5
- w_back: bfloat16 [4096, 1024], P(('ctx', 'fsdp')), may hold values from -0.125 to 0.125
- back_bias: bfloat16 [1024], P(('ctx', 'fsdp')), may hold values from -1.5 to 1.5
- cotangent: bfloat16 [8, 1024, 1024], P(('fsdp', 'rep'), 'ctx'), may hold values from -6 to 6
Outputs:
- layer_output: bfloat16 [8, 1024, 1024], P(('fsdp', 'rep'), 'ctx')
- input_grad: float32 [8, 1024, 1024], P(('fsdp', 'rep'), 'ctx')
- ln1_gain_grad: float32 [1024], P(('ctx', 'fsdp'))
- ln1_bias_grad: float32 [1024], P(('ctx', 'fsdp'))
- w_qkv_grad: float32 [1024, 3072], P(('ctx', 'fsdp'))
- q_bias_grad: float32 [1024], P(('ctx', 'fsdp'))
- v_bias_grad: float32 [1024], P(('ctx', 'fsdp'))
- w_out_grad: float32 [1024, 1024], P(('ctx', 'fsdp'))
- out_bias_grad: float32 [1024], P(('ctx', 'fsdp'))
- ln2_gain_grad: float32 [1024], P(('ctx', 'fsdp'))
- ln2_bias_grad: float32 [1024], P(('ctx', 'fsdp'))
- w_in_grad: float32 [1024, 4096], P(('ctx', 'fsdp'))
- in_bias_grad: float32 [4096], P(('ctx', 'fsdp'))
- w_back_grad: float32 [4096, 1024], P(('ctx', 'fsdp'))
- back_bias_grad: float32 [1024], P(('ctx', 'fsdp'))
Inputs may be any that keep to these rules, and one draw needn't show every extreme that they name: `segments`: segment numbers never fall along a sequence, every number of 0 to 4 occurs in each sequence, and some document of each sequence fills exactly 800 slots.
All inputs are finite; a program needn't handle non-finite values.
Results may differ from a plain program's by a relative error of at most 0.015.
Values may be sent and summed in bfloat16 or wider, within the bound.
A program may use at most 192 MiB of HBM per device.

v0:
```python
import math

import jax
import jax.numpy as jnp
from jax import lax
from jax.sharding import PartitionSpec as P

H = 16
HD = 64


epsilon = 1e-05
masked_value = -1e30


def layer_norm(values, gain, shift):
    center = values - jnp.mean(values, -1, keepdims=True)
    spread = jnp.mean(center * center, -1, keepdims=True)
    return center * lax.rsqrt(spread + epsilon) * gain + shift


def gelu_tanh(pre_values):
    return jax.nn.gelu(pre_values, approximate=True)


def shards(
    tokens,
    segments,
    ln1_gain,
    ln1_bias,
    w_qkv,
    q_bias,
    v_bias,
    w_out,
    out_bias,
    ln2_gain,
    ln2_bias,
    w_in,
    in_bias,
    w_back,
    back_bias,
    cotangent,
):
    seq_count, tok_count, width = tokens.shape
    row_count = seq_count * tok_count
    head_count = H
    head_dim = HD
    score_scale = 1.0 / math.sqrt(HD)
    ctx_index = lax.axis_index("ctx")
    gain_one, shift_one, qkv_weight, query_bias, value_bias, proj_weight, proj_bias = (
        lax.all_gather(ln1_gain, ("ctx", "fsdp"), axis=0, tiled=True),
        lax.all_gather(ln1_bias, ("ctx", "fsdp"), axis=0, tiled=True),
        lax.all_gather(w_qkv, ("ctx", "fsdp"), axis=0, tiled=True),
        lax.all_gather(q_bias, ("ctx", "fsdp"), axis=0, tiled=True),
        lax.all_gather(v_bias, ("ctx", "fsdp"), axis=0, tiled=True),
        lax.all_gather(w_out, ("ctx", "fsdp"), axis=0, tiled=True),
        lax.all_gather(out_bias, ("ctx", "fsdp"), axis=0, tiled=True),
    )
    inputs = tokens.reshape(row_count, width).astype(jnp.float32)
    gain_one_f = gain_one.astype(jnp.float32)
    shift_one_f = shift_one.astype(jnp.float32)
    normed_one = layer_norm(inputs, gain_one_f, shift_one_f).astype(jnp.bfloat16)
    projected = jnp.dot(normed_one, qkv_weight, preferred_element_type=jnp.float32)
    queries = (projected[:, :width] + query_bias.astype(jnp.float32)).astype(jnp.bfloat16)
    queries = queries.reshape(seq_count, tok_count, head_count, head_dim)
    key_rows = (
        projected[:, width : 2 * width].astype(jnp.bfloat16).reshape(seq_count, tok_count, width)
    )
    value_rows = (projected[:, 2 * width :] + value_bias.astype(jnp.float32)).astype(jnp.bfloat16)
    value_rows = value_rows.reshape(seq_count, tok_count, width)
    all_keys, all_values = (
        lax.all_gather(key_rows, "ctx", axis=1, tiled=True),
        lax.all_gather(value_rows, "ctx", axis=1, tiled=True),
    )
    key_count = all_keys.shape[1]
    all_keys = all_keys.reshape(seq_count, key_count, head_count, head_dim)
    all_values = all_values.reshape(seq_count, key_count, head_count, head_dim)
    query_pos = ctx_index * tok_count + jnp.arange(tok_count, dtype=jnp.int32)
    key_pos = jnp.arange(key_count, dtype=jnp.int32)
    query_seg = lax.dynamic_slice_in_dim(segments, ctx_index * tok_count, tok_count, 1)
    allowed = (query_seg[:, :, None] == segments[:, None, :]) & (
        key_pos[None, None, :] <= query_pos[None, :, None]
    )
    allowed = allowed[:, None]

    def masked_scores():
        raw_scores = jnp.einsum(
            "bqhd,bkhd->bhqk", queries, all_keys, preferred_element_type=jnp.float32
        )
        return jnp.where(allowed, raw_scores * score_scale, masked_value)

    scores = masked_scores()
    row_max = jnp.max(scores, -1, keepdims=True)
    exp_scores = jnp.exp(scores - row_max)
    row_total = jnp.sum(exp_scores, -1, keepdims=True)
    log_total = row_max + jnp.log(row_total)
    probs_low = (exp_scores / row_total).astype(jnp.bfloat16)
    attended = jnp.einsum(
        "bhqk,bkhd->bqhd", probs_low, all_values, preferred_element_type=jnp.float32
    )
    attended = attended.reshape(row_count, width).astype(jnp.bfloat16)
    branch = jnp.dot(attended, proj_weight, preferred_element_type=jnp.float32) + proj_bias.astype(
        jnp.float32
    )
    resid = inputs + branch
    gain_two, shift_two, up_weight, up_bias, down_weight, down_bias = (
        lax.all_gather(ln2_gain, ("ctx", "fsdp"), axis=0, tiled=True),
        lax.all_gather(ln2_bias, ("ctx", "fsdp"), axis=0, tiled=True),
        lax.all_gather(w_in, ("ctx", "fsdp"), axis=0, tiled=True),
        lax.all_gather(in_bias, ("ctx", "fsdp"), axis=0, tiled=True),
        lax.all_gather(w_back, ("ctx", "fsdp"), axis=0, tiled=True),
        lax.all_gather(back_bias, ("ctx", "fsdp"), axis=0, tiled=True),
    )
    gain_two_f = gain_two.astype(jnp.float32)
    shift_two_f = shift_two.astype(jnp.float32)
    normed_two = layer_norm(resid, gain_two_f, shift_two_f).astype(jnp.bfloat16)
    pre_act = jnp.dot(normed_two, up_weight, preferred_element_type=jnp.float32) + up_bias.astype(
        jnp.float32
    )
    activated = gelu_tanh(pre_act).astype(jnp.bfloat16)
    mixed_rows = (
        resid
        + jnp.dot(activated, down_weight, preferred_element_type=jnp.float32)
        + down_bias.astype(jnp.float32)
    )
    layer_output = mixed_rows.astype(jnp.bfloat16).reshape(seq_count, tok_count, width)
    gain_two_g, shift_two_g, up_back, down_back = (
        lax.all_gather(ln2_gain, ("ctx", "fsdp"), axis=0, tiled=True),
        lax.all_gather(ln2_bias, ("ctx", "fsdp"), axis=0, tiled=True),
        lax.all_gather(w_in, ("ctx", "fsdp"), axis=0, tiled=True),
        lax.all_gather(w_back, ("ctx", "fsdp"), axis=0, tiled=True),
    )
    gain_two_back = gain_two_g.astype(jnp.float32)
    shift_two_back = shift_two_g.astype(jnp.float32)
    g_output = cotangent.reshape(row_count, width)
    back_bias_grad = jnp.sum(g_output, 0, dtype=jnp.float32)
    w_back_grad = jnp.einsum("rf,rd->fd", activated, g_output, preferred_element_type=jnp.float32)
    g_act = jnp.einsum("rd,fd->rf", g_output, down_back, preferred_element_type=jnp.float32)
    gelu_pull = jax.vjp(gelu_tanh, pre_act)[1]
    g_pre = gelu_pull(g_act)[0].astype(jnp.bfloat16)
    in_bias_grad = jnp.sum(g_pre, 0, dtype=jnp.float32)
    w_in_grad = jnp.einsum("rd,rf->df", normed_two, g_pre, preferred_element_type=jnp.float32)
    g_normed_two = jnp.einsum("rf,df->rd", g_pre, up_back, preferred_element_type=jnp.float32)
    norm_two_pull = jax.vjp(layer_norm, resid, gain_two_back, shift_two_back)[1]
    g_resid_norm, ln2_gain_grad, ln2_bias_grad = norm_two_pull(g_normed_two)
    g_resid = g_output.astype(jnp.float32) + g_resid_norm
    mlp_sums = (
        lax.psum_scatter(ln2_gain_grad, ("ctx", "fsdp"), scatter_dimension=0, tiled=True),
        lax.psum_scatter(ln2_bias_grad, ("ctx", "fsdp"), scatter_dimension=0, tiled=True),
        lax.psum_scatter(w_in_grad, ("ctx", "fsdp"), scatter_dimension=0, tiled=True),
        lax.psum_scatter(in_bias_grad, ("ctx", "fsdp"), scatter_dimension=0, tiled=True),
        lax.psum_scatter(w_back_grad, ("ctx", "fsdp"), scatter_dimension=0, tiled=True),
        lax.psum_scatter(back_bias_grad, ("ctx", "fsdp"), scatter_dimension=0, tiled=True),
    )
    gain_one_g, shift_one_g, qkv_back, proj_back = (
        lax.all_gather(ln1_gain, ("ctx", "fsdp"), axis=0, tiled=True),
        lax.all_gather(ln1_bias, ("ctx", "fsdp"), axis=0, tiled=True),
        lax.all_gather(w_qkv, ("ctx", "fsdp"), axis=0, tiled=True),
        lax.all_gather(w_out, ("ctx", "fsdp"), axis=0, tiled=True),
    )
    gain_one_back = gain_one_g.astype(jnp.float32)
    shift_one_back = shift_one_g.astype(jnp.float32)
    g_branch = g_resid.astype(jnp.bfloat16)
    out_bias_grad = jnp.sum(g_branch, 0, dtype=jnp.float32)
    w_out_grad = jnp.einsum("rd,re->de", attended, g_branch, preferred_element_type=jnp.float32)
    g_attended = jnp.einsum("re,de->rd", g_branch, proj_back, preferred_element_type=jnp.float32)
    g_attended = g_attended.astype(jnp.bfloat16).reshape(seq_count, tok_count, head_count, head_dim)
    probs_back = jnp.exp(masked_scores() - log_total)
    probs_back_low = probs_back.astype(jnp.bfloat16)
    g_probs = jnp.einsum(
        "bqhd,bkhd->bhqk", g_attended, all_values, preferred_element_type=jnp.float32
    )
    row_dot = jnp.sum(probs_back * g_probs, -1, keepdims=True)
    g_scores = (probs_back * (g_probs - row_dot)).astype(jnp.bfloat16)
    g_queries = (
        jnp.einsum("bhqk,bkhd->bqhd", g_scores, all_keys, preferred_element_type=jnp.float32)
        * score_scale
    )
    g_queries = g_queries.astype(jnp.bfloat16).reshape(row_count, width)
    key_part = (
        jnp.einsum("bhqk,bqhd->bkhd", g_scores, queries, preferred_element_type=jnp.float32)
        * score_scale
    )
    value_part = jnp.einsum(
        "bhqk,bqhd->bkhd", probs_back_low, g_attended, preferred_element_type=jnp.float32
    )
    key_grad, value_grad = (
        lax.psum_scatter(
            key_part.reshape(seq_count, key_count, width).astype(jnp.bfloat16),
            "ctx",
            scatter_dimension=1,
            tiled=True,
        ).astype(jnp.float32),
        lax.psum_scatter(
            value_part.reshape(seq_count, key_count, width).astype(jnp.bfloat16),
            "ctx",
            scatter_dimension=1,
            tiled=True,
        ).astype(jnp.float32),
    )
    key_low = key_grad.astype(jnp.bfloat16).reshape(row_count, width)
    value_low = value_grad.astype(jnp.bfloat16).reshape(row_count, width)
    q_bias_grad = jnp.sum(g_queries, 0, dtype=jnp.float32)
    v_bias_grad = jnp.sum(value_low, 0, dtype=jnp.float32)
    g_projected = jnp.concatenate([g_queries, key_low, value_low], axis=1)
    w_qkv_grad = jnp.einsum(
        "rd,re->de", normed_one, g_projected, preferred_element_type=jnp.float32
    )
    g_normed_one = jnp.einsum(
        "re,de->rd", g_projected, qkv_back, preferred_element_type=jnp.float32
    )
    norm_one_pull = jax.vjp(layer_norm, inputs, gain_one_back, shift_one_back)[1]
    g_input_norm, ln1_gain_grad, ln1_bias_grad = norm_one_pull(g_normed_one)
    input_grad = (g_resid + g_input_norm).reshape(seq_count, tok_count, width)
    attention_sums = (
        lax.psum_scatter(ln1_gain_grad, ("ctx", "fsdp"), scatter_dimension=0, tiled=True),
        lax.psum_scatter(ln1_bias_grad, ("ctx", "fsdp"), scatter_dimension=0, tiled=True),
        lax.psum_scatter(w_qkv_grad, ("ctx", "fsdp"), scatter_dimension=0, tiled=True),
        lax.psum_scatter(q_bias_grad, ("ctx", "fsdp"), scatter_dimension=0, tiled=True),
        lax.psum_scatter(v_bias_grad, ("ctx", "fsdp"), scatter_dimension=0, tiled=True),
        lax.psum_scatter(w_out_grad, ("ctx", "fsdp"), scatter_dimension=0, tiled=True),
        lax.psum_scatter(out_bias_grad, ("ctx", "fsdp"), scatter_dimension=0, tiled=True),
    )
    (
        sum_gain_one,
        sum_shift_one,
        sum_qkv,
        sum_query_bias,
        sum_value_bias,
        sum_proj,
        sum_proj_bias,
    ) = attention_sums
    sum_gain_two, sum_shift_two, sum_up, sum_up_bias, sum_down, sum_down_bias = mlp_sums
    summed = (
        lax.psum(sum_gain_one.astype(jnp.bfloat16), "rep").astype(jnp.float32),
        lax.psum(sum_shift_one.astype(jnp.bfloat16), "rep").astype(jnp.float32),
        lax.psum(sum_qkv.astype(jnp.bfloat16), "rep").astype(jnp.float32),
        lax.psum(sum_query_bias.astype(jnp.bfloat16), "rep").astype(jnp.float32),
        lax.psum(sum_value_bias.astype(jnp.bfloat16), "rep").astype(jnp.float32),
        lax.psum(sum_proj.astype(jnp.bfloat16), "rep").astype(jnp.float32),
        lax.psum(sum_proj_bias.astype(jnp.bfloat16), "rep").astype(jnp.float32),
        lax.psum(sum_gain_two.astype(jnp.bfloat16), "rep").astype(jnp.float32),
        lax.psum(sum_shift_two.astype(jnp.bfloat16), "rep").astype(jnp.float32),
        lax.psum(sum_up.astype(jnp.bfloat16), "rep").astype(jnp.float32),
        lax.psum(sum_up_bias.astype(jnp.bfloat16), "rep").astype(jnp.float32),
        lax.psum(sum_down.astype(jnp.bfloat16), "rep").astype(jnp.float32),
        lax.psum(sum_down_bias.astype(jnp.bfloat16), "rep").astype(jnp.float32),
    )
    return (
        layer_output,
        input_grad,
        summed[0],
        summed[1],
        summed[2],
        summed[3],
        summed[4],
        summed[5],
        summed[6],
        summed[7],
        summed[8],
        summed[9],
        summed[10],
        summed[11],
        summed[12],
    )


def solution(mesh):
    in_specs = (
        P(("fsdp", "rep"), "ctx", None),
        P(("fsdp", "rep"), None),
        P(("ctx", "fsdp")),
        P(("ctx", "fsdp")),
        P(("ctx", "fsdp"), None),
        P(("ctx", "fsdp")),
        P(("ctx", "fsdp")),
        P(("ctx", "fsdp"), None),
        P(("ctx", "fsdp")),
        P(("ctx", "fsdp")),
        P(("ctx", "fsdp")),
        P(("ctx", "fsdp"), None),
        P(("ctx", "fsdp")),
        P(("ctx", "fsdp"), None),
        P(("ctx", "fsdp")),
        P(("fsdp", "rep"), "ctx", None),
    )
    out_specs = (
        P(("fsdp", "rep"), "ctx", None),
        P(("fsdp", "rep"), "ctx", None),
        P(("ctx", "fsdp")),
        P(("ctx", "fsdp")),
        P(("ctx", "fsdp"), None),
        P(("ctx", "fsdp")),
        P(("ctx", "fsdp")),
        P(("ctx", "fsdp"), None),
        P(("ctx", "fsdp")),
        P(("ctx", "fsdp")),
        P(("ctx", "fsdp")),
        P(("ctx", "fsdp"), None),
        P(("ctx", "fsdp")),
        P(("ctx", "fsdp"), None),
        P(("ctx", "fsdp")),
    )
    return jax.shard_map(shards, mesh=mesh, in_specs=in_specs, out_specs=out_specs, check_vma=False)
```

profile of v0, /device:TPU:29, one launch (start us, length us, event | category | flops | bytes accessed | tf_op | source)
XLA Modules:
  0.0 1085.4 jit_solution(18061836639881474800)
XLA Ops:
  8.0 1.3 fusion.58
  10.0 0.8 dynamic-update-slice.6
  10.8 0.8 dynamic-update-slice.7
  11.6 0.8 dynamic-update-slice.4
  12.5 0.8 dynamic-update-slice.3
  13.3 0.8 dynamic-update-slice.2
  14.2 0.8 dynamic-update-slice
  15.0 0.8 dynamic-update-slice.1
  15.8 0.8 dynamic-update-slice.5
  16.7 60.2 %all-reduce.18 = (bf16[1024]{0:T(1024)(128)(2,1)S(1)}, bf16[1024]{0:T(1024)(128)(2,1)S(1)}, bf16[1024]{0:T(1024)(128)(2,1)S(1)}, bf16[1024]{0:T(1024)(128)(2,1)S...) all-reduce(bf16[1024]{0:T(1024)(128)(2,1)S(1)} %dynamic-update-slic, ...), channel_id=1, replica_groups=mesh['ctx'=4,'fsdp'=4,'rep'=2] {'ctx','fsdp'}, use_global_device_ids=true, to_apply=%add.1 | all-reduce | flops 8192 | bytes 32768
  76.8 1.2 convert_reduce_fusion.2
  78.0 1.3 fusion.32
  79.4 4.9 fusion.51
  84.4 1.2 fusion.34
  85.7 0.9 slice.23
  88.4 30.1 %all-gather.2 = bf16[16,1,256]{2,1,0:T(2,128)(2,1)S(1)} all-gather(bf16[1,1,256]{2,1,0:T(2,128)(2,1)S(1)} %reshape.365), channel_id=1, replica_groups=mesh['ctx'=4,'fsdp'=4,'rep'=2] {'ctx','fsdp'}, dimensions={0}, use_global_device_ids=true | all-gather | bytes 8704 | tf_op jit(solution)/shard_map/all_gather | solution.py:110
  118.9 1.3 copy.44
  120.3 4.0 copy.43
  124.3 10.7 all-gather.20.cloned.1.call-done
  134.9 2.9 copy.45
  137.8 3.0 fusion.59
  140.9 3.8 fusion
  144.7 2.6 copy-done
  147.3 4.3 fusion.25
  151.6 25.6 %all-gather.12.cloned.1.call-done = bf16[1024,1024]{1,0:T(8,128)(2,1)} async-done(((bf16[64,1024]{1,0:T(8,128)(2,1)}), bf16[1024,1024]{1,0:T(8,128)(2,1)}) %all-gather.12.cloned.1.call-update) | async-done | bytes 2097168 | tf_op jit(solution)/shard_map/all_gather | solution.py:56
  177.2 2.4 fusion.60
  180.0 72.2 %all-gather.14.cloned.1.call-done = bf16[1024,4096]{1,0:T(8,128)(2,1)} async-done(((bf16[64,4096]{1,0:T(8,128)(2,1)}), bf16[1024,4096]{1,0:T(8,128)(2,1)}) %all-gather.14.cloned.1.call-update) | async-done | bytes 8388624 | tf_op jit(solution)/shard_map/all_gather | solution.py:109
  252.2 8.0 convolution_add_fusion
  260.2 67.0 %all-gather.16.cloned.1.call-done = bf16[4096,1024]{1,0:T(8,128)(2,1)} async-done(((bf16[256,1024]{1,0:T(8,128)(2,1)}), bf16[4096,1024]{1,0:T(8,128)(2,1)}) %all-gather.16.cloned.1.call-update) | async-done | bytes 8388624 | tf_op jit(solution)/shard_map/all_gather | solution.py:111
  327.2 12.3 %convert_reduce_fusion = (f32[4096]{0:T(1024)}, bf16[256,4096]{1,0:T(8,128)(2,1)S(1)}) fusion(f32[256,4096]{1,0:T(8,128)} %convolution_add_fusion, bf16[4096,1024]{1,0:T(8,128)(2,1)} %all-gather.16.cloned.1.call-done, bf16[1,256,1024]{2,1,0:T(8,128)(2,1)S(1)} %copy-done.11), kind=kOutput, calls=%fused_computation.21 | convolution fusion | flops 2170548224 | bytes 15220736 | tf_op jit(solution)/shard_map/rd,fd->rf/dot_general | solution.py:138
  339.5 1.4 copy-done.20
  340.8 3.2 multiply_reduce_fusion.1
  344.5 0.8 convert_reduce_fusion.3
  345.3 0.8 copy-done.18
  347.1 9.2 fusion.13
  356.4 10.0 multiply_reduce_fusion
  366.3 7.7 multiply_convert_fusion
  374.1 3.5 multiply_convert_fusion.1
  378.1 2.7 fusion.61
  381.2 1.1 copy-done.4
  382.4 6.2 convert_reduce_fusion.5
  388.5 32.2 %reduce-scatter.7.cloned.1.call-done = bf16[1,256,1024]{1,2,0:T(8,128)(2,1)} async-done(((bf16[1,1024,1024]{1,2,0:T(8,128)(2,1)}), bf16[1,256,1024]{1,2,0:T(8,128)(2,1)}) %reduce-scatter.7.cloned.1.call-update) | async-done | bytes 524304 | tf_op jit(solution)/shard_map/reduce_scatter | solution.py:188
  420.8 7.7 fusion.38
  428.6 1.0 copy-done.13
  429.5 11.7 %fusion.40 = f32[4096,1024]{1,0:T(8,128)} fusion(bf16[1,256,1024]{2,1,0:T(8,128)(2,1)S(1)} %copy-done.13, f32[256,4096]{1,0:T(8,128)} %convolution_add_fusion), kind=kOutput, calls=%fused_computation.72 | convolution fusion | flops 2156920832 | bytes 21495808 | tf_op jit(solution)/shard_map/rf,rd->fd/dot_general | solution.py:137
  441.3 1.2 copy-done.6
  442.5 9.9 fusion.54
  454.1 8.7 fusion.26
  463.0 32.0 %reduce-scatter.13.cloned.1.call-done = f32[64,1024]{1,0:T(8,128)} async-done(((f32[1024,1024]{1,0:T(8,128)}), f32[64,1024]{1,0:T(8,128)}) %reduce-scatter.13.cloned.1.call-update) | async-done | bytes 262160 | tf_op jit(solution)/shard_map/reduce_scatter | solution.py:221
  495.0 1.6 convert_element_type.286
  496.6 137.6 %reduce-scatter.11.cloned.1.call-done = f32[64,3072]{1,0:T(8,128)} async-done(((f32[1024,3072]{1,0:T(8,128)}), f32[64,3072]{1,0:T(8,128)}) %reduce-scatter.11.cloned.1.call-update) | async-done | bytes 786448 | tf_op jit(solution)/shard_map/reduce_scatter | solution.py:218
  634.2 1.9 convert_element_type.278
  636.1 178.6 %reduce-scatter.17.cloned.1.call-done = f32[256,1024]{1,0:T(8,128)} async-done(((f32[4096,1024]{1,0:T(8,128)}), f32[256,1024]{1,0:T(8,128)}) %reduce-scatter.17.cloned.1.call-update) | async-done | bytes 1048592 | tf_op jit(solution)/shard_map/reduce_scatter | solution.py:152
  814.7 2.1 convert_element_type.300
  816.8 178.3 %reduce-scatter.15.cloned.1.call-done = f32[64,4096]{1,0:T(8,128)} async-done(((f32[1024,4096]{1,0:T(8,128)}), f32[64,4096]{1,0:T(8,128)}) %reduce-scatter.15.cloned.1.call-update) | async-done | bytes 1048592 | tf_op jit(solution)/shard_map/reduce_scatter | solution.py:150
  995.1 2.1 convert_element_type.295
  997.3 4.9 fusion.55
  1002.8 1.5 convert_reduce_fusion.1
  1004.3 57.5 %all-reduce.17 = (bf16[1024]{0:T(1024)(128)(2,1)S(1)}, bf16[1024]{0:T(1024)(128)(2,1)S(1)}, bf16[1024]{0:T(1024)(128)(2,1)S(1)}, bf16[1024]{0:T(1024)(128)(2,1)S...) all-reduce(f32[1024]{0:T(1024)S(1)} %get-tuple-element.17, ...), channel_id=6, replica_groups=mesh['ctx'=4,'fsdp'=4,'rep'=2] {'ctx','fsdp'}, use_global_device_ids=true, to_apply=%region_14.15.clone | all-reduce | flops 12288 | bytes 73728
  1062.5 3.8 all-reduce.19
  1071.0 1.6 convert_element_type.287
  1072.6 1.9 convert_element_type.279
  1074.5 2.1 convert_element_type.296
  1076.6 2.1 convert_element_type.301
  (169 shorter events, 12.4 us)
Async XLA Ops:
  7.2 72.2 %all-gather.10.cloned.1.call-start = ((), (), s32[]{:S(2)}) async-start(), calls=%async_computation.6 | async-start | bytes 6684672 | tf_op jit(solution)/shard_map/all_gather | solution.py:53
  7.9 112.3 %all-gather.18.cloned.1.call-start = ((), (), s32[]{:S(2)}) async-start(), calls=%async_computation.16 | async-start | bytes 2621440 | tf_op jit(solution)/shard_map/all_gather | solution.py:73
  78.0 6.3 copy-start.25
  79.4 5.0 copy-start.35
  79.4 4.9 copy-start.29
  84.3 4.0 copy-start.44
  84.4 34.2 %copy-start.39 = (s32[1,1024]{1,0:T(1,128)S(1)}, s32[1,1024]{1,0:T(1,128)}, u32[]{:S(2)}) copy-start(s32[1,1024]{1,0:T(1,128)} %param.17) | copy-start | bytes 12292
  85.6 49.3 %all-gather.20.cloned.1.call-start = ((), (), s32[]{:S(2)}) async-start(), calls=%async_computation.17 | async-start | bytes 2621440 | tf_op jit(solution)/shard_map/all_gather | solution.py:72
  86.6 90.6 %all-gather.12.cloned.1.call-start = ((), (), s32[]{:S(2)}) async-start(), calls=%async_computation.7 | async-start | bytes 2228224 | tf_op jit(solution)/shard_map/all_gather | solution.py:56
  87.1 165.0 %all-gather.14.cloned.1.call-start = ((), (), s32[]{:S(2)}) async-start(), calls=%async_computation.8 | async-start | bytes 8912896 | tf_op jit(solution)/shard_map/all_gather | solution.py:109
  87.7 239.4 %all-gather.16.cloned.1.call-start = ((), (), s32[]{:S(2)}) async-start(), calls=%async_computation.9 | async-start | bytes 8912896 | tf_op jit(solution)/shard_map/all_gather | solution.py:111
  88.3 300.2 %reduce-scatter.9.cloned.1.call-start = ((), (), s32[]{:S(2)}) async-start(), calls=%async_computation.11 | async-start | bytes 2621440 | tf_op jit(solution)/shard_map/reduce_scatter | solution.py:194
  88.4 163.8 %copy-start.23 = (f32[1024]{0:T(1024)}, f32[1024]{0:T(1024)S(1)}, u32[]{:S(2)}) copy-start(f32[1024]{0:T(1024)S(1)} %convert_element_type.251) | copy-start | bytes 12292
  137.8 3.1 copy-start.3
  140.9 6.5 copy-start
  140.9 6.4 copy-start.9
  147.3 29.9 %copy-start.2 = (bf16[1,256,1024]{2,1,0:T(8,128)(2,1)S(1)}, bf16[1,256,1024]{2,1,0:T(8,128)(2,1)}, u32[]{:S(2)}) copy-start(bf16[1,256,1024]{2,1,0:T(8,128)(2,1)} %param.16) | copy-start | bytes 1572868
  151.6 100.6 %copy-start.14 = (bf16[16,64,256]{2,1,0:T(8,128)(2,1)}, bf16[16,64,256]{2,1,0:T(8,128)(2,1)S(1)}, u32[]{:S(2)}) copy-start(bf16[16,64,256]{2,1,0:T(8,128)(2,1)S(1)} %fusion.25) | copy-start | bytes 1572868
  179.6 164.4 %copy-start.5 = (f32[256,1024]{1,0:T(8,128)}, f32[256,1024]{1,0:T(8,128)S(1)}, u32[]{:S(2)}) copy-start(f32[256,1024]{1,0:T(8,128)S(1)} %get-tuple-element.65) | copy-start | bytes 3145732
  179.6 164.4 %copy-start.27 = (f32[256]{0:T(256)}, f32[256]{0:T(256)S(1)}, u32[]{:S(2)}) copy-start(f32[256]{0:T(256)S(1)} %broadcast_multiply_fusion) | copy-start | bytes 3076
  179.9 164.1 %copy-start.31 = (f32[256]{0:T(256)}, f32[256]{0:T(256)S(1)}, u32[]{:S(2)}) copy-start(f32[256]{0:T(256)S(1)} %fusion.47) | copy-start | bytes 3076
  179.9 167.1 %copy-start.22 = (f32[16,256]{1,0:T(8,128)}, f32[16,256]{1,0:T(8,128)S(1)}, u32[]{:S(2)}) copy-start(f32[16,256]{1,0:T(8,128)S(1)} %log_add_fusion) | copy-start | bytes 49156
  252.2 75.0 %copy-start.11 = (bf16[1,256,1024]{2,1,0:T(8,128)(2,1)S(1)}, bf16[1,256,1024]{2,1,0:T(8,128)(2,1)}, u32[]{:S(2)}) copy-start(bf16[1,256,1024]{2,1,0:T(8,128)(2,1)} %param.31) | copy-start | bytes 1572868
  327.2 13.7 %copy-start.43 = (bf16[1024,4096]{1,0:T(8,128)(2,1)S(1)}, bf16[1024,4096]{1,0:T(8,128)(2,1)}, u32[]{:S(2)}) copy-start(bf16[1024,4096]{1,0:T(8,128)(2,1)} %all-gather.14.cloned.1.call-done) | copy-start | bytes 25165828
  339.5 1.4 copy-start.20
  340.8 3.6 copy-start.12
  344.0 2.1 copy-start.16
  344.4 11.9 %copy-start.7 = (f32[256,1024]{1,0:T(8,128)}, f32[256,1024]{1,0:T(8,128)S(1)}, u32[]{:S(2)}) copy-start(f32[256,1024]{1,0:T(8,128)S(1)} %get-tuple-element.55) | copy-start | bytes 3145732
  344.5 11.8 %copy-start.37 = (f32[256]{0:T(256)}, f32[256]{0:T(256)S(1)}, u32[]{:S(2)}) copy-start(f32[256]{0:T(256)S(1)} %negate_multiply_fusion.1) | copy-start | bytes 3076
  345.3 0.8 copy-start.18
  347.1 9.2 copy-start.10
  356.3 64.4 %reduce-scatter.7.cloned.1.call-start = ((), (), s32[]{:S(2)}) async-start(), calls=%async_computation.10 | async-start | bytes 2621440 | tf_op jit(solution)/shard_map/reduce_scatter | solution.py:188
  374.0 3.9 copy-start.1
  374.1 4.0 copy-start.15
  374.1 4.0 copy-start.19
  378.0 117.0 %reduce-scatter.13.cloned.1.call-start = ((), (), s32[]{:S(2)}) async-start(), calls=%async_computation.13 | async-start | bytes 4456448 | tf_op jit(solution)/shard_map/reduce_scatter | solution.py:221
  380.7 1.6 copy-start.4
  380.8 40.0 %copy-start.26 = (f32[256]{0:T(256)S(1)}, f32[256]{0:T(256)}, u32[]{:S(2)}) copy-start(f32[256]{0:T(256)} %copy-done.25) | copy-start | bytes 3076
  380.8 40.0 %copy-start.30 = (f32[256]{0:T(256)S(1)}, f32[256]{0:T(256)}, u32[]{:S(2)}) copy-start(f32[256]{0:T(256)} %copy-done.29) | copy-start | bytes 3076
  380.8 253.4 %reduce-scatter.11.cloned.1.call-start = ((), (), s32[]{:S(2)}) async-start(), calls=%async_computation.12 | async-start | bytes 13369344 | tf_op jit(solution)/shard_map/reduce_scatter | solution.py:218
  428.5 1.0 copy-start.13
  428.5 386.2 %reduce-scatter.17.cloned.1.call-start = ((), (), s32[]{:S(2)}) async-start(), calls=%async_computation.15 | async-start | bytes 17825792 | tf_op jit(solution)/shard_map/reduce_scatter | solution.py:152
  441.2 1.3 copy-start.6
  441.2 1.3 copy-start.24
  441.2 1.3 copy-start.28
  441.2 1.3 copy-start.32
  441.2 553.9 %reduce-scatter.15.cloned.1.call-start = ((), (), s32[]{:S(2)}) async-start(), calls=%async_computation.14 | async-start | bytes 17825792 | tf_op jit(solution)/shard_map/reduce_scatter | solution.py:150
  452.4 1.5 copy-start.42
  452.4 618.5 %all-reduce.23.cloned.1.call-start = ((), (), s32[]{:S(2)}) async-start(), calls=%async_computation.18 | async-start | bytes 3145728 | tf_op jit(solution)/shard_map/psum | solution.py:237
  454.1 8.7 copy-start.17
  462.8 534.5 %copy-start.21 = (bf16[1,256,1024]{1,2,0:T(8,128)(2,1)S(1)}, bf16[1,256,1024]{1,2,0:T(8,128)(2,1)}, u32[]{:S(2)}) copy-start(bf16[1,256,1024]{1,2,0:T(8,128)(2,1)} %reduce-scatter.7.cloned.1.call-done) | copy-start | bytes 1572868
  997.2 4.9 copy-start.36
  997.2 5.5 copy-start.8
  997.3 5.5 copy-start.38
  1002.1 2.2 copy-start.33
  1002.1 2.2 copy-start.34
  1002.1 2.2 copy-start.40
  1002.2 2.1 copy-start.41
Sparse Core Ops, SparseCore 0:
  10.3 62.3 all-gather.9
  85.7 24.4 all-gather.17
  112.3 22.5 all-gather.19
  137.0 40.1 all-gather.11
  179.3 72.8 all-gather.13
  254.3 72.8 all-gather.15
  356.4 30.5 reduce-scatter.8
  389.6 31.1 reduce-scatter.6
  424.6 70.3 reduce-scatter.12
  498.9 135.2 reduce-scatter.10
  638.3 176.3 reduce-scatter.16
  818.7 176.4 reduce-scatter.14
  998.7 51.2 all-reduce.22
where the time goes:
time: 1100 us; the launch traced here: 1090 us
  waiting for transfers between devices  737 us (67%)
  blocking collectives  152 us (14%)
  matrix products  113 us (10%)
  other arithmetic  39.6 us (4%)
  local copies, waits for them, and re-layouts  26.5 us (2%)
  between operations  16.7 us (2%)
    reduce_scatter x1, waiting for transfers between devices, shards(): lax.psum_scatter(w_back_grad, ('ctx', 'fsdp'), scatter_dimension=0, tiled...  179 us
    reduce_scatter x1, waiting for transfers between devices, shards(): lax.psum_scatter(w_in_grad, ('ctx', 'fsdp'), scatter_dimension=0, tiled=T...  178 us
    reduce_scatter x1, waiting for transfers between devices, shards(): lax.psum_scatter(w_qkv_grad, ('ctx', 'fsdp'), scatter_dimension=0, tiled=...  138 us
    unnamed x2, blocking collectives  118 us
    all_gather x1, waiting for transfers between devices, shards(): lax.all_gather(w_in, ('ctx', 'fsdp'), axis=0, tiled=True)  72.2 us
    all_gather x1, waiting for transfers between devices, shards(): lax.all_gather(w_back, ('ctx', 'fsdp'), axis=0, tiled=True)  67 us
    reduce_scatter x1, waiting for transfers between devices, shards(): lax.psum_scatter(key_part.reshape(seq_count, key_count, width).astype(jnp...  32.2 us
    reduce_scatter x1, waiting for transfers between devices, shards(): lax.psum_scatter(w_out_grad, ('ctx', 'fsdp'), scatter_dimension=0, tiled=...  32 us
  transfers between devices with their start and end apart: 13, of which 9 were waited for; matrix products, arithmetic and copies ran while one was open for 12% of the time, Pallas kernels for 0%

commit v1 on v0

v1 whole, which is shorter than its diff:
```python
import math

import jax
import jax.numpy as jnp
from jax import lax
from jax.sharding import PartitionSpec as P

H = 16
HD = 64
EPS = 1e-05
MASKED = -1e30
F32, BF16 = jnp.float32, jnp.bfloat16
OWN = ("ctx", "fsdp")


def dot(a, b, dims):
    return lax.dot_general(a, b, (dims, ((), ())), preferred_element_type=F32)


def norm_parts(x):
    center = x - jnp.mean(x, -1, keepdims=True)
    rstd = lax.rsqrt(jnp.mean(center * center, -1, keepdims=True) + EPS)
    return center * rstd, rstd


def norm_back(g, z, rstd, gain):
    gz = g * gain
    return rstd * (gz - jnp.mean(gz, -1, keepdims=True) - z * jnp.mean(gz * z, -1, keepdims=True))


def ctx_gather(x):
    return lax.all_gather(x, "ctx", axis=0, tiled=True)


def ctx_scatter(x):
    return lax.psum_scatter(x.astype(BF16), "ctx", scatter_dimension=0, tiled=True).astype(F32)


def shards(n, tokens, segments, ln1_gain, ln1_bias, w_qkv, q_bias, v_bias, w_out, out_bias,
           ln2_gain, ln2_bias, w_in, in_bias, w_back, back_bias, cotangent):
    own_rows, width = tokens.shape[1], tokens.shape[2]
    rows_in = w_qkv.shape[0]
    heads = H // n
    cols = heads * HD
    ctx = lax.axis_index("ctx")
    small = jnp.stack([ln1_gain, ln1_bias, q_bias, v_bias, out_bias, ln2_gain, ln2_bias, back_bias])
    small = lax.all_gather(small, OWN, axis=1, tiled=True).astype(F32)
    gain1, bias1, qb, vb, ob, gain2, bias2, bb = [small[i] for i in range(8)]
    qb = lax.dynamic_slice_in_dim(qb, ctx * cols, cols)
    vb = lax.dynamic_slice_in_dim(vb, ctx * cols, cols)
    inb = lax.all_gather(in_bias, "fsdp", axis=0, tiled=True).astype(F32)
    wq = lax.all_to_all(w_qkv.reshape(rows_in, 3, n, cols), "ctx", 2, 0)
    wq = lax.all_gather(wq.reshape(n, rows_in, 3 * cols), "fsdp", axis=1, tiled=True).reshape(width, 3 * cols)
    wo = lax.all_gather(w_out, "fsdp", axis=0, tiled=True)
    ffc = w_in.shape[1] // n
    wi = lax.all_to_all(w_in.reshape(rows_in, n, ffc), "ctx", 1, 0)
    wi = lax.all_gather(wi, "fsdp", axis=1, tiled=True).reshape(width, ffc)
    wb = lax.all_gather(w_back, "fsdp", axis=0, tiled=True)

    x = tokens[0].astype(F32)
    cot = cotangent[0]
    z1, rstd1 = norm_parts(x)
    n1 = ctx_gather((z1 * gain1 + bias1).astype(BF16))
    cot_all = ctx_gather(cot)
    proj = dot(n1, wq, ((1,), (0,)))
    slots = n1.shape[0]
    q = (proj[:, :cols] + qb).astype(BF16).reshape(slots, heads, HD)
    k = proj[:, cols:2 * cols].astype(BF16).reshape(slots, heads, HD)
    v = (proj[:, 2 * cols:] + vb).astype(BF16).reshape(slots, heads, HD)
    seg = segments[0]
    pos = jnp.arange(slots)
    allowed = ((seg[:, None] == seg[None, :]) & (pos[None, :] <= pos[:, None]))[None]
    scale = 1.0 / math.sqrt(HD)
    s = jnp.einsum("qhd,khd->hqk", q, k, preferred_element_type=F32)
    s = jnp.where(allowed, s * scale, MASKED)
    m = jnp.max(s, -1, keepdims=True)
    e = jnp.exp(s - m)
    probs = e / jnp.sum(e, -1, keepdims=True)
    pl_ = probs.astype(BF16)
    att = jnp.einsum("hqk,khd->qhd", pl_, v, preferred_element_type=F32).astype(BF16).reshape(slots, cols)
    resid = x + ctx_scatter(dot(att, wo, ((1,), (0,)))) + ob
    z2, rstd2 = norm_parts(resid)
    n2 = ctx_gather((z2 * gain2 + bias2).astype(BF16))
    pre = dot(n2, wi, ((1,), (0,))) + inb
    gelu = lambda t: jax.nn.gelu(t, approximate=True)
    act_f, pull = jax.vjp(gelu, pre)
    act = act_f.astype(BF16)
    g_pre = pull(dot(cot_all, wb, ((1,), (1,))))[0].astype(BF16)
    g_n2 = ctx_scatter(dot(g_pre, wi, ((1,), (1,))))
    out = resid + ctx_scatter(dot(act, wb, ((1,), (0,)))) + bb
    g_wb = dot(act, cot_all, ((0,), (0,)))
    g_wi = dot(n2, g_pre, ((0,), (0,)))
    g_inb = jnp.sum(g_pre, 0, dtype=F32)
    cot_f = cot.astype(F32)
    g_bb = jnp.sum(cot_f, 0)
    g_gain2, g_bias2 = jnp.sum(g_n2 * z2, 0), jnp.sum(g_n2, 0)
    g_resid = cot_f + norm_back(g_n2, z2, rstd2, gain2)
    gb_own = g_resid.astype(BF16)
    gb = ctx_gather(gb_own)
    g_ob = jnp.sum(gb_own, 0, dtype=F32)
    g_wo = dot(att, gb, ((0,), (0,)))
    g_att = dot(gb, wo, ((1,), (1,))).astype(BF16).reshape(slots, heads, HD)
    g_p = jnp.einsum("qhd,khd->hqk", g_att, v, preferred_element_type=F32)
    g_s = (probs * (g_p - jnp.sum(probs * g_p, -1, keepdims=True))).astype(BF16)
    g_q = (jnp.einsum("hqk,khd->qhd", g_s, k, preferred_element_type=F32) * scale).astype(BF16)
    g_k = (jnp.einsum("hqk,qhd->khd", g_s, q, preferred_element_type=F32) * scale).astype(BF16)
    g_v = jnp.einsum("hqk,qhd->khd", pl_, g_att, preferred_element_type=F32).astype(BF16)
    g_proj = jnp.concatenate([t.reshape(slots, cols) for t in (g_q, g_k, g_v)], 1)
    g_qb, g_vb = jnp.sum(g_proj[:, :cols], 0, dtype=F32), jnp.sum(g_proj[:, 2 * cols:], 0, dtype=F32)
    g_n1 = ctx_scatter(dot(g_proj, wq, ((1,), (1,))))
    g_wq = dot(n1, g_proj, ((0,), (0,)))
    g_gain1, g_bias1 = jnp.sum(g_n1 * z1, 0), jnp.sum(g_n1, 0)
    g_x = g_resid + norm_back(g_n1, z1, rstd1, gain1)

    def owners(g):
        return lax.psum_scatter(g.astype(BF16), "fsdp", scatter_dimension=0, tiled=True)

    def by_rows(g, parts):
        g = g.astype(BF16).reshape(n, -1, g.shape[1])
        g = lax.psum_scatter(g, "fsdp", scatter_dimension=1, tiled=True)
        g = lax.all_to_all(g, "ctx", 0, 0)
        g = g.reshape(n, rows_in, parts, -1).transpose(1, 2, 0, 3)
        return g.reshape(rows_in, -1)

    grads = [by_rows(g_wq, 3), owners(g_wo), by_rows(g_wi, 1), owners(g_wb)]
    grads = [lax.psum(g, "rep").astype(F32) for g in grads]
    spread = lambda g: lax.dynamic_update_slice_in_dim(jnp.zeros((width,), F32), g, ctx * cols, 0)
    vec = jnp.stack([g_gain1, g_bias1, spread(g_qb), spread(g_vb), g_ob, g_gain2, g_bias2, g_bb])
    vec = lax.psum(lax.psum_scatter(vec, OWN, scatter_dimension=1, tiled=True), "rep")
    g_inb = lax.psum(lax.psum_scatter(g_inb, "fsdp", scatter_dimension=0, tiled=True), "rep")
    return (out.astype(BF16)[None], g_x[None], vec[0], vec[1], grads[0], vec[2], vec[3], grads[1],
            vec[4], vec[5], vec[6], grads[2], g_inb, grads[3], vec[7])


def solution(mesh):
    own, rows = P(OWN), P(OWN, None)
    seqs = P(("fsdp", "rep"), "ctx", None)
    in_specs = (seqs, P(("fsdp", "rep"), None), own, own, rows, own, own, rows, own, own, own, rows, own, rows, own, seqs)
    out_specs = (seqs, seqs, own, own, rows, own, own, rows, own, own, own, rows, own, rows, own)
    n = mesh.shape["ctx"]
    body = lambda *args: shards(n, *args)
    return jax.shard_map(body, mesh=mesh, in_specs=in_specs, out_specs=out_specs, check_vma=False)
```

time: 1100 us -> 707 us (0.64)
  waiting for transfers between devices: 737 us -> 425 us
  blocking collectives: 152 us -> 80 us
  starting transfers between devices: 1.1 us -> 18.3 us
    reduce_scatter x6 -> x8, waiting for transfers between devices: 559 us -> 170 us  [the longest x4 103 us: ctx_scatter(): lax.psum_scatter(x.astype(BF16), 'ctx', scatter_dimension=0, tiled=True)]
    unnamed x2 -> x1, blocking collectives: 118 us -> 7.72 us
    psum x1, waiting for transfers between devices: 0.01 us -> 49.9 us  [shards(): grads = [lax.psum(g, 'rep').astype(F32) for g in grads]]
    unnamed x13 -> x18, waiting for transfers between devices: 2.41 us -> 50.2 us
    all_gather x6 -> x7, waiting for transfers between devices: 175 us -> 147 us  [the longest x4 74.5 us: ctx_gather(): return lax.all_gather(x, 'ctx', axis=0, tiled=True)]
    all_to_all x0 -> x2, blocking collectives: none -> 20.1 us  [the longest x1 10.5 us: shards(): wi = lax.all_to_all(w_in.reshape(rows_in, n, ffc), 'ctx', 1, 0)]
    all_gather x1 -> x3, blocking collectives: 30.1 us -> 47.9 us  [the longest x1 29.2 us: shards(): small = lax.all_gather(small, OWN, axis=1, tiled=True).astype(F32)]
    dot_general x18 -> x17, matrix products: 113 us -> 96.3 us  [the longest x12 60.8 us: dot(): return lax.dot_general(a, b, (dims, ((), ())), preferred_element_type=F32)]
  transfers between devices with their start and end apart: 13 -> 19, of which waited for: 9 -> 16; matrix products, arithmetic and copies ran while one was open for 12% -> 15% of each run, Pallas kernels for 0% -> 0%
where the time goes in v1:
time: 707 us; the launch traced here: 695 us
  waiting for transfers between devices  425 us (60%)
  matrix products  106 us (15%)
  blocking collectives  80 us (11%)
  other arithmetic  32.6 us (5%)
  starting transfers between devices  18.3 us (3%)
  local copies, waits for them, and re-layouts  16.9 us (2%)
  between operations  15.5 us (2%)
    reduce_scatter x4, waiting for transfers between devices, ctx_scatter(): lax.psum_scatter(x.astype(BF16), 'ctx', scatter_dimension=0, tiled=True)  103 us
    all_gather x4, waiting for transfers between devices, ctx_gather(): return lax.all_gather(x, 'ctx', axis=0, tiled=True)  74.5 us
    dot_general x12, matrix products, dot(): return lax.dot_general(a, b, (dims, ((), ())), preferred_element_type=F32)  60.8 us
    reduce_scatter x2, waiting for transfers between devices, owners(): lax.psum_scatter(g.astype(BF16), 'fsdp', scatter_dimension=0, tiled=True)  58.4 us
    unnamed x18, waiting for transfers between devices  50.2 us
    psum x1, waiting for transfers between devices, shards(): grads = [lax.psum(g, 'rep').astype(F32) for g in grads]  49.9 us
    all_gather x1, waiting for transfers between devices, shards(): wb = lax.all_gather(w_back, 'fsdp', axis=0, tiled=True)  38.7 us
    all_gather x1, waiting for transfers between devices, shards(): wi = lax.all_gather(wi, 'fsdp', axis=1, tiled=True).reshape(width, ffc)  34 us
  transfers between devices with their start and end apart: 19, of which 16 were waited for; matrix products, arithmetic and copies ran while one was open for 15% of the time, Pallas kernels for 0%

profile of v1, /device:TPU:29, one launch (start us, length us, event | category | flops | bytes accessed | tf_op | source)
XLA Modules:
  0.0 694.7 jit_solution(11439857501506292630)
XLA Ops:
  7.3 1.4 broadcast_in_dim_reshape.6
  8.8 9.6 %all_to_all.40 = bf16[1,64,3,4,256]{4,1,2,0,3:T(8,128)(2,1)S(1)} all-to-all(bf16[1,64,3,4,256]{4,1,2,0,3:T(8,128)(2,1)S(1)} %copy.65), channel_id=1, replica_groups=mesh['ctx'=4,'fsdp'=4,'rep'=2] {'ctx'}, dimensions={3} | all-to-all | bytes 786432 | tf_op jit(solution)/shard_map/all_to_all | solution.py:52
  18.7 1.2 reshape_squeeze.3
  20.1 29.2 %all-gather.2 = bf16[16,64,8]{1,2,0:T(8,128)(2,1)S(1)} all-gather(bf16[1,64,8]{1,2,0:T(8,128)(2,1)S(1)} %bitcast.238), channel_id=1, replica_groups=mesh['ctx'=4,'fsdp'=4,'rep'=2] {'ctx','fsdp'}, dimensions={0}, use_global_device_ids=true | all-gather | bytes 17408 | tf_op jit(solution)/shard_map/all_gather | solution.py:47
  50.5 1.1 fusion.49
  51.7 13.0 %all_gather.33 = bf16[256,1024]{1,0:T(8,128)(2,1)S(1)} all-gather(bf16[64,1024]{1,0:T(8,128)(2,1)S(1)} %copy-done.13), channel_id=1, replica_groups=mesh['ctx'=4,'fsdp'=4,'rep'=2] {'fsdp'}, dimensions={0}, use_global_device_ids=true | all-gather | bytes 655360 | tf_op jit(solution)/shard_map/all_gather | solution.py:54
  65.4 17.1 %all-gather.12.cloned.1.call-done = bf16[1024,1024]{1,0:T(8,128)(2,1)} async-done(((bf16[256,1024]{1,0:T(8,128)(2,1)}), bf16[1024,1024]{1,0:T(8,128)(2,1)}) %all-gather.12.cloned.1.call-update) | async-done | bytes 2097168 | tf_op jit(solution)/shard_map/all_gather | solution.py:32
  82.5 3.9 fusion.74
  87.4 9.9 %fusion.73 = (f32[4,1024]{1,0:T(4,128)S(1)}, f32[4,1024,1024]{1,2,0:T(8,128)}) fusion(pred[1024,1024]{0,1:T(8,128)(4,1)S(1)} %fusion.16, bf16[1024,4,64]{0,2,1:T(8,128)(2,1)S(1)} %bitcast.199, bf16[1024,4,64]{0,2,1:T(8,128)(2,1)S(1)} %bitcast.192), kind=kOutput, calls=%fused_computation.124 | convolution fusion | flops 553649152 | bytes 18890752 | tf_op jit(solution)/shard_map/sub | solution.py:77
  97.3 7.5 %fusion.36 = bf16[4,64,1024]{2,1,0:T(8,128)(2,1)S(1)} fusion(bf16[1024,4,64]{0,2,1:T(8,128)(2,1)} %bitcast.213, f32[4,1024,1024]{1,2,0:T(8,128)} %get-tuple-element.52, f32[4,1024]{1,0:T(4,128)S(1)} %get-tuple-element.51), kind=kOutput, calls=%fused_computation.60 | convolution fusion | flops 545521664 | bytes 17842176 | tf_op jit(solution)/shard_map/hqk,khd->qhd/dot_general | solution.py:80
  104.9 2.1 convolution_convert_fusion.3
  107.6 10.5 %all_to_all.41 = bf16[1,64,4,1024]{3,1,0,2:T(8,128)(2,1)S(1)} all-to-all(bf16[1,64,4,1024]{3,1,0,2:T(8,128)(2,1)S(1)} %copy.68), channel_id=1, replica_groups=mesh['ctx'=4,'fsdp'=4,'rep'=2] {'ctx'}, dimensions={2} | all-to-all | bytes 1048576 | tf_op jit(solution)/shard_map/all_to_all | solution.py:56
  118.1 1.2 copy.69
  119.6 18.2 %reduce-scatter.12.cloned.1.call-done = bf16[256,1024]{1,0:T(8,128)(2,1)} async-done(((bf16[1024,1024]{1,0:T(8,128)(2,1)}), bf16[256,1024]{1,0:T(8,128)(2,1)}) %reduce-scatter.12.cloned.1.call-update) | async-done | bytes 524304 | tf_op jit(solution)/shard_map/reduce_scatter | solution.py:36
  137.8 1.3 fusion.66
  139.1 1.4 multiply_reduce_fusion.1
  140.5 2.2 add_convert_fusion.1
  144.1 5.6 all-gather.3
  149.7 34.0 %all-gather.22.cloned.1.call-done = bf16[4,1,256,1,1024]{4,0,3,1,2:T(4,128)(2,1)} async-done(((bf16[4,1,64,1,1024]{4,0,3,1,2:T(4,128)(2,1)}), bf16[4,1,256,1,1024]{4,0,3,1,2:T(4,128)(2,1)}) %all-gather.22.cloned.1.call-update) | async-done | bytes 2097168 | tf_op jit(solution)/shard_map/all_gather | solution.py:57
  183.6 2.2 copy.70
  185.9 23.5 %all-gather.16.cloned.1.call-done = bf16[1024,1024]{1,0:T(8,128)(2,1)} async-done(((bf16[256,1024]{1,0:T(8,128)(2,1)}), bf16[1024,1024]{1,0:T(8,128)(2,1)}) %all-gather.16.cloned.1.call-update) | async-done | bytes 2097168 | tf_op jit(solution)/shard_map/all_gather | solution.py:32
  209.4 6.0 fusion.75
  215.4 38.7 %all-gather.18.cloned.1.call-done = bf16[1024,1024]{1,0:T(8,128)(2,1)} async-done(((bf16[256,1024]{1,0:T(8,128)(2,1)}), bf16[1024,1024]{1,0:T(8,128)(2,1)}) %all-gather.18.cloned.1.call-update) | async-done | bytes 2097168 | tf_op jit(solution)/shard_map/all_gather | solution.py:58
  254.1 25.4 %all-gather.24.cloned.1.call-done = bf16[1,1024,1024]{2,1,0:T(8,128)(2,1)} async-done(((bf16[1,256,1024]{2,1,0:T(8,128)(2,1)}), bf16[1,1024,1024]{2,1,0:T(8,128)(2,1)}) %all-gather.24.cloned.1.call-update) | async-done | bytes 2097168 | tf_op jit(solution)/shard_map/all_gather | solution.py:32
  279.5 8.8 %convert_reduce_fusion = (f32[1024]{0:T(1024)}, bf16[1024,1024]{1,0:T(8,128)(2,1)S(1)}) fusion(f32[1024,1024]{1,0:T(8,128)} %fusion.75, f32[1024]{0:T(1024)S(1)} %bitcast.241, bf16[1024,1024]{1,0:T(8,128)(2,1)} %all-gather.18.cloned.1.call-done, bf16[1,1024,1024]{2,1,0:T(8,128)(2,1)} %all-gather.24.cloned.1.call-done), kind=kOutput, calls=%fused_computation.19 | convolution fusion | flops 2171599872 | bytes 10493952 | tf_op jit(solution)/shard_map/dot_general | solution.py:17
  288.3 1.3 copy-done.37
  289.6 3.8 convolution_convert_fusion.1
  293.5 7.1 %convolution_convert_fusion.2 = bf16[1024,1024]{1,0:T(8,128)(2,1)} fusion(bf16[1024,1024]{1,0:T(8,128)(2,1)} %all-gather.18.cloned.1.call-done, f32[1024,1024]{1,0:T(8,128)} %fusion.75, f32[1024]{0:T(1024)S(1)} %bitcast.242), kind=kOutput, calls=%fused_computation.35 | convolution fusion | flops 2159017984 | bytes 8392704 | tf_op jit(solution)/shard_map/dot_general | solution.py:17
  300.6 23.5 %reduce-scatter.16.cloned.1.call-done = bf16[256,1024]{1,0:T(8,128)(2,1)} async-done(((bf16[1024,1024]{1,0:T(8,128)(2,1)}), bf16[256,1024]{1,0:T(8,128)(2,1)}) %reduce-scatter.16.cloned.1.call-update) | async-done | bytes 524304 | tf_op jit(solution)/shard_map/reduce_scatter | solution.py:36
  324.2 2.3 fusion.61
  326.4 31.5 %reduce-scatter.14.cloned.1.call-done = bf16[256,1024]{1,0:T(8,128)(2,1)} async-done(((bf16[1024,1024]{1,0:T(8,128)(2,1)}), bf16[256,1024]{1,0:T(8,128)(2,1)}) %reduce-scatter.14.cloned.1.call-update) | async-done | bytes 524304 | tf_op jit(solution)/shard_map/reduce_scatter | solution.py:36
  357.9 3.5 convert_reduce_fusion.5
  361.5 6.0 convolution_convert_fusion
  367.5 8.8 %reduce-scatter.20.cloned.1.call-start = ((), (), s32[]{:S(2)}) async-start(), calls=%async_computation.22 | async-start | bytes 1966080 | tf_op jit(solution)/shard_map/reduce_scatter | solution.py:120
  376.3 8.4 %all-gather.20.cloned.1.call-done = bf16[1024,1024]{1,0:T(8,128)(2,1)} async-done(((bf16[256,1024]{1,0:T(8,128)(2,1)}), bf16[1024,1024]{1,0:T(8,128)(2,1)}) %all-gather.20.cloned.1.call-update) | async-done | bytes 2097168 | tf_op jit(solution)/shard_map/all_gather | solution.py:32
  384.7 3.1 convolution_convert_fusion.7
  387.8 16.8 %multiply_reduce_fusion = (f32[4,1024]{1,0:T(4,128)}, f32[4,1024,1024]{1,2,0:T(8,128)}) fusion(f32[4,1024,1024]{1,2,0:T(8,128)} %get-tuple-element.52, f32[4,1024]{1,0:T(4,128)} %copy-done.14, bf16[1024,4,64]{0,2,1:T(8,128)(2,1)} %bitcast.254, bf16[1024,4,64]{0,2,1:T(8,128)(2,1)} %bitcast.214), kind=kOutput, calls=%fused_computation.2 | convolution fusion | flops 549449728 | bytes 34635776 | tf_op jit(solution)/shard_map/qhd,khd->hqk/dot_general | solution.py:103
  404.7 8.0 %multiply_convert_fusion = bf16[4,1024,1024]{1,2,0:T(8,128)(2,1)S(1)} fusion(f32[4,1024,1024]{1,2,0:T(8,128)} %get-tuple-element.54, f32[4,1024]{1,0:T(4,128)} %get-tuple-element.53, f32[4,1024,1024]{1,2,0:T(8,128)S(1)} %bitcast.191, f32[4,1024]{1,0:T(4,128)} %copy-done.14), kind=kLoop, calls=%fused_computation.1 | loop fusion | flops 16777216 | bytes 41975808 | tf_op jit(solution)/shard_map/convert_element_type | solution.py:104
  412.7 3.5 fusion.43
  416.2 2.4 convert_reduce_fusion.7
  418.6 5.3 convert_reduce_fusion.6
  423.9 4.9 convolution_convert_fusion.5
  428.9 4.8 convolution_convert_fusion.4
  434.0 7.2 %fusion.25 = bf16[1024,1024]{1,0:T(8,128)(2,1)} fusion(bf16[1,1024,1024]{2,1,0:T(8,128)(2,1)} %all-gather.24.cloned.1.call-done, f32[1024,1024]{1,0:T(8,128)} %fusion.75, f32[1024]{0:T(1024)S(1)} %bitcast.243), kind=kOutput, calls=%fused_computation.32 | convolution fusion | flops 2159017984 | bytes 8392704 | tf_op jit(solution)/shard_map/dot_general | solution.py:17
  441.3 3.1 convolution_convert_fusion.6
  444.5 3.7 all-to-all-start.3
  448.4 7.7 %all-to-all-done.3 = bf16[4,64,1024]{2,1,0:T(8,128)(2,1)S(1)} async-done(((bf16[4,64,1024]{2,1,0:T(8,128)(2,1)}), bf16[4,64,1024]{2,1,0:T(8,128)(2,1)S(1)}, u32[]{:S(2)}, u32[]{:S(2)}) %all-to-all-start.3) | async-done | bytes 524320 | tf_op jit(solution)/shard_map/all_to_all | solution.py:121
  456.1 8.8 %reduce-scatter.20.cloned.1.call-done = bf16[4,64,768]{2,1,0:T(8,128)(2,1)} async-done(((bf16[4,256,768]{2,1,0:T(8,128)(2,1)}), bf16[4,64,768]{2,1,0:T(8,128)(2,1)}) %reduce-scatter.20.cloned.1.call-update) | async-done | bytes 393232 | tf_op jit(solution)/shard_map/reduce_scatter | solution.py:120
  464.9 4.8 all-to-all-start.2
  469.8 29.7 %reduce-scatter.18.cloned.1.call-done = bf16[256,1024]{1,0:T(8,128)(2,1)} async-done(((bf16[1024,1024]{1,0:T(8,128)(2,1)}), bf16[256,1024]{1,0:T(8,128)(2,1)}) %reduce-scatter.18.cloned.1.call-update) | async-done | bytes 524304 | tf_op jit(solution)/shard_map/reduce_scatter | solution.py:36
  499.5 1.7 fusion.62
  503.7 1.5 reshape.191
  505.7 1.1 reshape.192
  506.8 36.8 %reduce-scatter.26.cloned.1.call-done = bf16[256,1024]{1,0:T(8,128)(2,1)} async-done(((bf16[1024,1024]{1,0:T(8,128)(2,1)}), bf16[256,1024]{1,0:T(8,128)(2,1)}) %reduce-scatter.26.cloned.1.call-update) | async-done | bytes 524304 | tf_op jit(solution)/shard_map/reduce_scatter | solution.py:116
  543.6 21.6 %reduce-scatter.22.cloned.1.call-done = bf16[64,1024]{1,0:T(8,128)(2,1)} async-done(((bf16[256,1024]{1,0:T(8,128)(2,1)}), bf16[64,1024]{1,0:T(8,128)(2,1)}) %reduce-scatter.22.cloned.1.call-update) | async-done | bytes 131088 | tf_op jit(solution)/shard_map/reduce_scatter | solution.py:116
  566.5 7.7 %all-reduce = f32[1024]{0:T(1024)S(1)} all-reduce(f32[1024]{0:T(1024)S(1)} %copy-done.23), channel_id=12, replica_groups=mesh['ctx'=4,'fsdp'=4,'rep'=2] {'fsdp'}, use_global_device_ids=true, to_apply=%region_32.33.clone | all-reduce | flops 1024 | bytes 8192
  574.4 1.4 fusion.53
  575.7 48.8 %reduce-scatter.28.cloned.1.call-done = f32[64,8]{1,0:T(8,128)} async-done(((f32[1024,8]{1,0:T(8,128)}), f32[64,8]{1,0:T(8,128)}) %reduce-scatter.28.cloned.1.call-update) | async-done | bytes 2064
  625.3 4.4 all-reduce.1
  630.2 49.9 %all-reduce.5.cloned.1.call-done = (bf16[64,3072]{1,0:T(8,128)(2,1)}, bf16[64,1024]{1,0:T(8,128)(2,1)}, bf16[64,4096]{1,0:T(8,128)(2,1)}, bf16[256,1024]{1,0:T(8,128)(2,1)}) async-done(((bf16[64,3072]{1,0:T(8,128)(2,1)}, bf16[64,1024]{1,0:T(8,128)(2,1)}, bf16[64,4096]{1,0:T(8,128)(2,1)}, bf16[256,1024]{1,0:T(8,128)(2,1)}), (bf16[64,3072]{1,0:T(8,128)(2,1)}, bf16[64,1024]{1,0:T(8,128)(2,1)}, ...) | async-done | bytes 1572880 | tf_op jit(solution)/shard_map/psum | solution.py:126
  680.1 1.6 convert_element_type.173
  681.8 1.9 convert_element_type.171
  683.7 2.1 convert_element_type.175
  685.8 2.1 convert_element_type.178
  (160 shorter events, 11.8 us)
Async XLA Ops:
  7.2 12.8 %copy-start.34 = (bf16[64]{0:T(256)(128)(2,1)S(1)}, bf16[64]{0:T(256)(128)(2,1)}, u32[]{:S(2)}) copy-start(bf16[64]{0:T(256)(128)(2,1)} %param.30) | copy-start | bytes 388
  7.2 12.8 %copy-start.33 = (bf16[64]{0:T(256)(128)(2,1)S(1)}, bf16[64]{0:T(256)(128)(2,1)}, u32[]{:S(2)}) copy-start(bf16[64]{0:T(256)(128)(2,1)} %param.26) | copy-start | bytes 388
  7.2 12.8 %copy-start.32 = (bf16[64]{0:T(256)(128)(2,1)S(1)}, bf16[64]{0:T(256)(128)(2,1)}, u32[]{:S(2)}) copy-start(bf16[64]{0:T(256)(128)(2,1)} %param.25) | copy-start | bytes 388
  7.2 12.8 %copy-start.31 = (bf16[64]{0:T(256)(128)(2,1)S(1)}, bf16[64]{0:T(256)(128)(2,1)}, u32[]{:S(2)}) copy-start(bf16[64]{0:T(256)(128)(2,1)} %param.24) | copy-start | bytes 388
  7.2 12.8 %copy-start.30 = (bf16[64]{0:T(256)(128)(2,1)S(1)}, bf16[64]{0:T(256)(128)(2,1)}, u32[]{:S(2)}) copy-start(bf16[64]{0:T(256)(128)(2,1)} %param.22) | copy-start | bytes 388
  7.2 12.8 %copy-start.29 = (bf16[64]{0:T(256)(128)(2,1)S(1)}, bf16[64]{0:T(256)(128)(2,1)}, u32[]{:S(2)}) copy-start(bf16[64]{0:T(256)(128)(2,1)} %param.21) | copy-start | bytes 388
  7.2 12.8 %copy-start.28 = (bf16[64]{0:T(256)(128)(2,1)S(1)}, bf16[64]{0:T(256)(128)(2,1)}, u32[]{:S(2)}) copy-start(bf16[64]{0:T(256)(128)(2,1)} %param.19) | copy-start | bytes 388
  7.3 12.8 %copy-start.27 = (bf16[64]{0:T(256)(128)(2,1)S(1)}, bf16[64]{0:T(256)(128)(2,1)}, u32[]{:S(2)}) copy-start(bf16[64]{0:T(256)(128)(2,1)} %param.18) | copy-start | bytes 388
  7.3 42.2 %copy-start = (bf16[1,256,1024]{2,1,0:T(8,128)(2,1)S(1)}, bf16[1,256,1024]{2,1,0:T(8,128)(2,1)}, u32[]{:S(2)}) copy-start(bf16[1,256,1024]{2,1,0:T(8,128)(2,1)} %param.16) | copy-start | bytes 1572868
  7.3 44.4 %copy-start.13 = (bf16[64,1024]{1,0:T(8,128)(2,1)S(1)}, bf16[64,1024]{1,0:T(8,128)(2,1)}, u32[]{:S(2)}) copy-start(bf16[64,1024]{1,0:T(8,128)(2,1)} %param.23) | copy-start | bytes 393220
  7.3 57.5 %copy-start.15 = (s32[1,1024]{1,0:T(1,128)S(1)}, s32[1,1024]{1,0:T(1,128)}, u32[]{:S(2)}) copy-start(s32[1,1024]{1,0:T(1,128)} %param.17) | copy-start | bytes 12292
  7.3 58.1 %all-gather.14.cloned.1.call-start = ((), (), s32[]{:S(2)}) async-start(), calls=%async_computation.14 | async-start | bytes 1966080 | tf_op jit(solution)/shard_map/all_gather | solution.py:53
  19.9 62.6 %all-gather.12.cloned.1.call-start = ((), (), s32[]{:S(2)}) async-start(), calls=%async_computation.13 | async-start | bytes 2621440 | tf_op jit(solution)/shard_map/all_gather | solution.py:32
  49.9 1.8 copy-start.17
  51.6 86.2 %reduce-scatter.12.cloned.1.call-start = ((), (), s32[]{:S(2)}) async-start(), calls=%async_computation.15 | async-start | bytes 2621440 | tf_op jit(solution)/shard_map/reduce_scatter | solution.py:36
  64.7 40.2 %copy-start.3 = (bf16[256,1024]{1,0:T(8,128)(2,1)}, bf16[256,1024]{1,0:T(8,128)(2,1)S(1)}, u32[]{:S(2)}) copy-start(bf16[256,1024]{1,0:T(8,128)(2,1)S(1)} %all_gather.33) | copy-start | bytes 1572868
  87.4 9.9 %copy-start.5 = (bf16[1024,256]{0,1:T(8,128)(2,1)}, bf16[1024,256]{0,1:T(8,128)(2,1)S(1)}, u32[]{:S(2)}) copy-start(bf16[1024,256]{0,1:T(8,128)(2,1)S(1)} %get-tuple-element.32) | copy-start | bytes 1572868
  97.3 7.5 %copy-start.14 = (f32[4,1024]{1,0:T(4,128)}, f32[4,1024]{1,0:T(4,128)S(1)}, u32[]{:S(2)}) copy-start(f32[4,1024]{1,0:T(4,128)S(1)} %get-tuple-element.51) | copy-start | bytes 49156
  104.9 13.2 %copy-start.11 = (bf16[4,64,1024]{2,1,0:T(8,128)(2,1)}, bf16[4,64,1024]{2,1,0:T(8,128)(2,1)S(1)}, u32[]{:S(2)}) copy-start(bf16[4,64,1024]{2,1,0:T(8,128)(2,1)S(1)} %fusion.36) | copy-start | bytes 1572868
  104.9 2.2 copy-start.10
  107.0 76.6 %all-gather.22.cloned.1.call-start = ((), (), s32[]{:S(2)}) async-start(), calls=%async_computation.26 | async-start | bytes 2621440 | tf_op jit(solution)/shard_map/all_gather | solution.py:57
  107.6 36.4 %copy-start.35 = (bf16[256]{0:T(256)(128)(2,1)S(1)}, bf16[256]{0:T(256)(128)(2,1)}, u32[]{:S(2)}) copy-start(bf16[256]{0:T(256)(128)(2,1)} %param.28) | copy-start | bytes 1540
  119.3 90.1 %all-gather.16.cloned.1.call-start = ((), (), s32[]{:S(2)}) async-start(), calls=%async_computation.16 | async-start | bytes 2621440 | tf_op jit(solution)/shard_map/all_gather | solution.py:32
  140.5 183.7 %copy-start.22 = (f32[256]{0:T(256)}, f32[256]{0:T(256)S(1)}, u32[]{:S(2)}) copy-start(f32[256]{0:T(256)S(1)} %add_rsqrt_fusion) | copy-start | bytes 3076
  142.7 111.4 %all-gather.18.cloned.1.call-start = ((), (), s32[]{:S(2)}) async-start(), calls=%async_computation.17 | async-start | bytes 2621440 | tf_op jit(solution)/shard_map/all_gather | solution.py:58
  143.2 136.2 %all-gather.24.cloned.1.call-start = ((), (), s32[]{:S(2)}) async-start(), calls=%async_computation.27 | async-start | bytes 2621440 | tf_op jit(solution)/shard_map/all_gather | solution.py:32
  144.0 180.2 %reduce-scatter.16.cloned.1.call-start = ((), (), s32[]{:S(2)}) async-start(), calls=%async_computation.19 | async-start | bytes 2621440 | tf_op jit(solution)/shard_map/reduce_scatter | solution.py:36
  149.7 143.8 %copy-start.24 = (f32[4,1,256]{2,1,0:T(1,128)}, f32[4,1,256]{2,1,0:T(1,128)S(1)}, u32[]{:S(2)}) copy-start(f32[4,1,256]{2,1,0:T(1,128)S(1)} %convert_element_type.181) | copy-start | bytes 12292
  288.3 1.3 copy-start.37
  293.4 30.8 %copy-start.1 = (bf16[256,1024]{1,0:T(8,128)(2,1)S(1)}, bf16[256,1024]{1,0:T(8,128)(2,1)}, u32[]{:S(2)}) copy-start(bf16[256,1024]{1,0:T(8,128)(2,1)} %reduce-scatter.12.cloned.1.call-done) | copy-start | bytes 1572868
  293.4 64.5 %copy-start.2 = (bf16[1,256,1024]{2,1,0:T(8,128)(2,1)S(1)}, bf16[1,256,1024]{2,1,0:T(8,128)(2,1)}, u32[]{:S(2)}) copy-start(bf16[1,256,1024]{2,1,0:T(8,128)(2,1)} %param.31) | copy-start | bytes 1572868
  293.4 64.5 %copy-start.20 = (f32[1,1024]{1,0:T(1,128)S(1)}, f32[1,1024]{1,0:T(1,128)}, u32[]{:S(2)}) copy-start(f32[1,1024]{1,0:T(1,128)} %get-tuple-element.35) | copy-start | bytes 12292
  293.4 64.5 %reduce-scatter.14.cloned.1.call-start = ((), (), s32[]{:S(2)}) async-start(), calls=%async_computation.18 | async-start | bytes 2621440 | tf_op jit(solution)/shard_map/reduce_scatter | solution.py:36
  300.6 84.1 %all-gather.20.cloned.1.call-start = ((), (), s32[]{:S(2)}) async-start(), calls=%async_computation.20 | async-start | bytes 2621440 | tf_op jit(solution)/shard_map/all_gather | solution.py:32
  361.4 23.3 %copy-start.4 = (bf16[256,1024]{1,0:T(8,128)(2,1)S(1)}, bf16[256,1024]{1,0:T(8,128)(2,1)}, u32[]{:S(2)}) copy-start(bf16[256,1024]{1,0:T(8,128)(2,1)} %copy-done.3) | copy-start | bytes 1572868
  361.4 83.0 %reduce-scatter.24.cloned.1.call-start = ((), (), s32[]{:S(2)}) async-start(), calls=%async_computation.24 | async-start | bytes 2621440 | tf_op jit(solution)/shard_map/reduce_scatter | solution.py:120
  367.5 97.4 %reduce-scatter.20.cloned.1.call-start = ((), (), s32[]{:S(2)}) async-start(), calls=%async_computation.22 | async-start | bytes 1966080 | tf_op jit(solution)/shard_map/reduce_scatter | solution.py:120
  387.8 16.9 %slice-start = ((s8[16777216]{0:T(1024)(128)(4,1)}), s8[4194304]{0:T(1024)(128)(4,1)S(1)}, s32[]{:S(2)}) async-start(s8[16777216]{0:T(1024)(128)(4,1)} %bitcast.190), calls=%async_computation.30 | async-start | bytes 8388608
  387.8 16.9 %slice-start.1 = ((s8[16777216]{0:T(1024)(128)(4,1)}), s8[4194304]{0:T(1024)(128)(4,1)S(1)}, s32[]{:S(2)}) async-start(s8[16777216]{0:T(1024)(128)(4,1)} %bitcast.190), calls=%async_computation.31 | async-start | bytes 8388608
  387.8 16.9 %slice-start.2 = ((s8[16777216]{0:T(1024)(128)(4,1)}), s8[4194304]{0:T(1024)(128)(4,1)S(1)}, s32[]{:S(2)}) async-start(s8[16777216]{0:T(1024)(128)(4,1)} %bitcast.190), calls=%async_computation.32 | async-start | bytes 8388608
  387.8 16.9 %slice-start.3 = ((s8[16777216]{0:T(1024)(128)(4,1)}), s8[4194304]{0:T(1024)(128)(4,1)S(1)}, s32[]{:S(2)}) async-start(s8[16777216]{0:T(1024)(128)(4,1)} %bitcast.190), calls=%async_computation.33 | async-start | bytes 8388608
  404.7 8.0 %copy-start.6 = (bf16[1024,256]{0,1:T(8,128)(2,1)S(1)}, bf16[1024,256]{0,1:T(8,128)(2,1)}, u32[]{:S(2)}) copy-start(bf16[1024,256]{0,1:T(8,128)(2,1)} %copy-done.5) | copy-start | bytes 1572868
  418.6 5.3 copy-start.8
  423.9 5.0 copy-start.9
  428.8 5.1 copy-start.25
  428.8 70.7 %reduce-scatter.18.cloned.1.call-start = ((), (), s32[]{:S(2)}) async-start(), calls=%async_computation.21 | async-start | bytes 2621440 | tf_op jit(solution)/shard_map/reduce_scatter | solution.py:36
  433.7 7.6 %copy-start.12 = (bf16[4,64,1024]{2,1,0:T(8,128)(2,1)S(1)}, bf16[4,64,1024]{2,1,0:T(8,128)(2,1)}, u32[]{:S(2)}) copy-start(bf16[4,64,1024]{2,1,0:T(8,128)(2,1)} %copy-done.11) | copy-start | bytes 1572868
  433.7 109.9 %reduce-scatter.26.cloned.1.call-start = ((), (), s32[]{:S(2)}) async-start(), calls=%async_computation.25 | async-start | bytes 2621440 | tf_op jit(solution)/shard_map/reduce_scatter | solution.py:116
  441.2 7.0 %copy-start.26 = (f32[4,64]{1,0:T(4,128)S(1)}, f32[4,64]{1,0:T(4,128)}, u32[]{:S(2)}) copy-start(f32[4,64]{1,0:T(4,128)} %get-tuple-element.57) | copy-start | bytes 3076
  441.2 58.3 %copy-start.18 = (f32[256]{0:T(256)S(1)}, f32[256]{0:T(256)}, u32[]{:S(2)}) copy-start(f32[256]{0:T(256)} %copy-done.17) | copy-start | bytes 3076
  441.2 60.0 %copy-start.16 = (f32[1024]{0:T(1024)S(1)}, f32[1024]{0:T(1024)}, u32[]{:S(2)}) copy-start(f32[1024]{0:T(1024)} %get-tuple-element.21) | copy-start | bytes 12292
  441.2 60.0 %copy-start.21 = (f32[1024]{0:T(1024)S(1)}, f32[1024]{0:T(1024)}, u32[]{:S(2)}) copy-start(f32[1024]{0:T(1024)} %get-tuple-element.29) | copy-start | bytes 12292
  441.2 124.0 %reduce-scatter.22.cloned.1.call-start = ((), (), s32[]{:S(2)}) async-start(), calls=%async_computation.23 | async-start | bytes 655360 | tf_op jit(solution)/shard_map/reduce_scatter | solution.py:116
  444.5 11.6 %all-to-all-start.3 = ((bf16[4,64,1024]{2,1,0:T(8,128)(2,1)}), bf16[4,64,1024]{2,1,0:T(8,128)(2,1)S(1)}, u32[]{:S(2)}, u32[]{:S(2)}) async-start(bf16[4,64,1024]{2,1,0:T(8,128)(2,1)} %reduce-scatter.24.cloned.1.call-done), calls=%async_computation.10 | async-start | bytes 1048576 | tf_op jit(solution)/shard_map/all_to_all | solution.py:121
  464.9 38.8 %all-to-all-start.2 = ((bf16[4,64,768]{2,1,0:T(8,128)(2,1)}), bf16[4,64,768]{2,1,0:T(8,128)(2,1)}, u32[]{:S(2)}, u32[]{:S(2)}) async-start(bf16[4,64,768]{2,1,0:T(8,128)(2,1)} %reduce-scatter.20.cloned.1.call-done), calls=%async_computation.7 | async-start | bytes 786432 | tf_op jit(solution)/shard_map/all_to_all | solution.py:121
  469.8 154.7 %reduce-scatter.28.cloned.1.call-start = ((), (), s32[]{:S(2)}) async-start(), calls=%async_computation.28 | async-start | bytes 557056
  469.8 95.5 %copy-start.36 = (u32[32]{0:T(128)S(1)}, u32[32]{0:T(128)}, u32[]{:S(2)}) copy-start(u32[32]{0:T(128)} %constant.54) | copy-start | bytes 388
  469.8 96.8 %copy-start.23 = (f32[1024]{0:T(1024)S(1)}, f32[1024]{0:T(1024)}, u32[]{:S(2)}) copy-start(f32[1024]{0:T(1024)} %get-tuple-element.59) | copy-start | bytes 12292
  469.8 104.6 %copy-start.19 = (f32[256]{0:T(256)S(1)}, f32[256]{0:T(256)}, u32[]{:S(2)}) copy-start(f32[256]{0:T(256)} %copy-done.17) | copy-start | bytes 3076
  499.5 74.8 %copy-start.7 = (bf16[256,1024]{1,0:T(8,128)(2,1)S(1)}, bf16[256,1024]{1,0:T(8,128)(2,1)}, u32[]{:S(2)}) copy-start(bf16[256,1024]{1,0:T(8,128)(2,1)} %reduce-scatter.18.cloned.1.call-done) | copy-start | bytes 1572868
  502.3 177.8 %all-reduce.5.cloned.1.call-start = ((), (), s32[]{:S(2)}) async-start(), calls=%async_computation.29 | async-start | bytes 3145728 | tf_op jit(solution)/shard_map/psum | solution.py:126
Sparse Core Ops, SparseCore 0:
  20.1 35.9 all-gather.13
  58.2 24.2 all-gather.11
  107.1 30.6 reduce-scatter.11
  139.8 43.8 all-gather.21
  185.6 23.7 all-gather.15
  210.8 43.2 all-gather.17
  255.6 23.7 all-gather.23
  293.5 30.6 reduce-scatter.15
  326.7 31.1 reduce-scatter.13
  361.5 23.1 all-gather.19
  387.0 41.3 reduce-scatter.23
  430.5 34.3 reduce-scatter.19
  467.4 32.0 reduce-scatter.17
  501.7 41.9 reduce-scatter.25
  546.3 18.8 reduce-scatter.21
  569.2 55.2 reduce-scatter.27
  627.4 52.7 all-reduce.4

commit v2 on v1

v2 whole, which is shorter than its diff:
```python
import functools

import jax
import jax.numpy as jnp
from jax import lax
from jax.experimental import pallas as pl
from jax.experimental.pallas import tpu as pltpu
from jax.sharding import PartitionSpec as P

H = 16
HD = 64
DOCS = 5
EPS = 1e-05
MASKED = -1e30
F32, BF16 = jnp.float32, jnp.bfloat16
MESH = pl.DeviceIdType.MESH
NN = ((1,), (0,))
NT = ((1,), (1,))
TN = ((0,), (0,))
QKV, OUT, IN, BACK = range(4)
CHUNK = 32


def dot(a, b, dims):
    return lax.dot_general(a, b, (dims, ((), ())), preferred_element_type=F32)


def norm_parts(x):
    center = x - jnp.mean(x, -1, keepdims=True)
    rstd = lax.rsqrt(jnp.mean(center * center, -1, keepdims=True) + EPS)
    return center * rstd, rstd


def norm_back(g, z, rstd, gain):
    gz = g * gain
    return rstd * (gz - jnp.mean(gz, -1, keepdims=True) - z * jnp.mean(gz * z, -1, keepdims=True))


def gelu_both(t):
    a, b = 0.7978845608028654, 0.044715
    t2 = t * t
    th = jnp.tanh(a * t * (1.0 + b * t2))
    half = 0.5 * (1.0 + th)
    return t * half, half + 0.5 * t * (1.0 - th * th) * (a * (1.0 + 3.0 * b * t2))


def fold(x):
    return jnp.sum(x.reshape(x.shape[0] // 8, 8, x.shape[1]), 0)


def body(dims, tok, cot_in, seg, pack, wq_hbm, wo_hbm, wi_hbm, wb_hbm,
         out_o, gx_o, gq_o, go_o, gi_o, gb_o, gv_o,
         wq, wo, wi, wb, packs, vecs, inb, n1, cot, n2, gbr, q_s, k_s, v_s, do_s, kt_s, vt_s, att, act, gpre, gproj,
         start_s, lse_s, delta_s, resid, gres, keep, tmp1, tmp2, snd, land,
         dk_s, dv_s, gwq, gwo, gwi, gwb, yq, yo, yi, yb, zq, zo, zi, zb, fq, fi, aq, ao, ai, ab,
         v6, v6r, vs, vy, vs2, vz, ibg, sums,
         loc, pk_cs, pk_cr, pk_zs, pk_zr, wc_s, wc_r, wz_s, wz_r, wy_s, wy_r, ag_s, ag_r, rs_s, rs_r,
         gy_s, gy_r, gz_s, gz_r, gc_s, gc_r, gf_s, gf_r, vc_s, vc_r, vy_s, vy_r, vz_s, vz_r):
    n, nf, t_rows, width, rows, brows, ffc = dims
    half_w, half_f = width // 2, ffc // 2
    hc = width // n
    pw = hc // 2
    c, f, r = lax.axis_index("ctx"), lax.axis_index("fsdp"), lax.axis_index("rep")
    x, core = c // 2, c % 2

    def rel(d):
        return ((x + d // 2) % 2) * 2 + (core + d % 2) % 2

    def on_ctx(d):
        return (rel(d), f, r)

    def on_z(f2):
        return (c, f2, r)

    on_y = (c, f, 1 - r)
    ends = []

    def make(src, dst, ss, rs, dev):
        return pltpu.make_async_remote_copy(src_ref=src, dst_ref=dst, send_sem=ss, recv_sem=rs, device_id=dev,
                                            device_id_type=MESH)

    def send(src, dst, ss, rs, dev, cond=None):
        if cond is None:
            make(src, dst, ss, rs, dev).start()
            ends.append(lambda: make(src, dst, ss, rs, dev).wait_send())
        else:
            @pl.when(cond)
            def _():
                make(src, dst, ss, rs, dev).start()

            def end():
                @pl.when(cond)
                def _():
                    make(src, dst, ss, rs, dev).wait_send()
            ends.append(end)

    def arrived(dst, rs, dev):
        make(dst, dst, rs, rs, dev).wait_recv()

    def local(src, dst, sem):
        pltpu.make_async_copy(src, dst, sem).start()

    def local_done(dst, sem):
        pltpu.make_async_copy(dst, dst, sem).wait()

    local(cot_in, cot.at[c], loc.at[0])
    for h in range(2):
        for j in range(3):
            local(wq_hbm.at[:, pl.ds(pl.multiple_of(j * width + c * hc + h * pw, pw), pw)],
                  wq.at[h, c, f, :, pl.ds(j * pw, pw)], loc.at[1])
        local(wo_hbm.at[:, pl.ds(h * half_w, half_w)], wo.at[h, f], loc.at[2])
        local(wi_hbm.at[:, pl.ds(pl.multiple_of(c * ffc + h * half_f, half_f), half_f)], wi.at[h, c, f], loc.at[3])
        local(wb_hbm.at[:, pl.ds(h * half_w, half_w)], wb.at[h, f], loc.at[4])
    packs[c, f] = pack[...]
    barrier = pltpu.get_barrier_semaphore()
    peers = [on_ctx(d) for d in (1, 2, 3)] + [on_z((f + s) % nf) for s in range(1, nf)] + [on_y]
    for dev in peers:
        pl.semaphore_signal(barrier, inc=1, device_id=dev, device_id_type=MESH)
    pl.semaphore_wait(barrier, len(peers))

    for d in (1, 2, 3):
        send(packs.at[c, f], packs.at[c, f], pk_cs.at[d], pk_cr.at[c], on_ctx(d))

    def exchange(kind, hbm, buf, parts, step, w):
        for d in (2, 3, 1):
            c2 = rel(d)
            for h in range(2):
                for j in range(parts):
                    make(hbm.at[:, pl.ds(pl.multiple_of(j * width + c2 * step + h * w, w), w)],
                         buf.at[h, c, f, :, pl.ds(j * w, w)], wc_s.at[kind, d], wc_r.at[kind, c], on_ctx(d)).start()
            ends.append(lambda d=d: make(buf.at[:, c, f], buf.at[:, c, f], wc_s.at[kind, d], wc_r.at[kind, c],
                                         on_ctx(d)).wait_send())

    def exchanged(kind, buf):
        for d in (1, 2, 3):
            arrived(buf.at[:, rel(d), f], wc_r.at[kind, rel(d)], on_ctx(d))

    exchange(0, wq_hbm, wq, 3, hc, pw)

    bufs = {QKV: wq, OUT: wo, IN: wi, BACK: wb}

    def block(buf, kind, h, f2):
        return buf.at[h, :, f2] if kind in (QKV, IN) else buf.at[h, f2]

    def w_send(kind, way, src, cond):
        nxt = f + 1 if way == 0 else f - 1
        b = block(bufs[kind], kind, r, src)
        send(b, b, wz_s.at[kind, way, src], wz_r.at[kind, src], on_z(nxt), cond)

    def w_own(kind):
        w_send(kind, 0, f, f + 1 < nf)
        w_send(kind, 1, f, f >= 1)

    def w_step(kind, s):
        for way in range(2):
            src = f - s if way == 0 else f + s
            ok = src >= 0 if way == 0 else src < nf
            b = block(bufs[kind], kind, r, src)

            @pl.when(ok)
            def _():
                arrived(b, wz_r.at[kind, src], on_y)
            w_send(kind, way, src, ok & ((f + 1 < nf) if way == 0 else (f >= 1)))
            send(b, b, wy_s.at[kind, src], wy_r.at[kind, src], on_y, ok)

    def w_arrived(kind):
        for s in range(1, nf):
            f2 = (f + s) % nf
            arrived(block(bufs[kind], kind, 1 - r, f2), wy_r.at[kind, f2], on_y)

    def ag_start(i, buf):
        for d, k in ((2, 0), (1, 1)):
            send(buf.at[c], buf.at[c], ag_s.at[i, k], ag_r.at[i, c], on_ctx(d))

    def ag_forward(i, buf):
        b = rel(2)
        arrived(buf.at[b], ag_r.at[i, b], on_ctx(2))
        send(buf.at[b], buf.at[b], ag_s.at[i, 2], ag_r.at[i, b], on_ctx(1))

    def ag_wait(i, buf, d):
        arrived(buf.at[rel(d)], ag_r.at[i, rel(d)], on_ctx(d))

    def rs_put(i, d, h, val):
        cols = pl.ds(h * half_w, half_w)
        if d == 0:
            keep[:, cols] = val
            return
        k = {3: 0, 2: 1, 1: 2}[d]
        if d == 2:
            arrived(land.at[i, 0, h], rs_r.at[i, 0, h], on_ctx(1))
            val = val + land[i, 0, h].astype(F32)
        snd[i % 2, k, h] = val.astype(BF16)
        make(snd.at[i % 2, k, h], land.at[i, k, h], rs_s.at[i, k, h], rs_r.at[i, k, h], on_ctx(2 if d == 2 else 1)).start()

    def rs_sent(i):
        for d, k in ((3, 0), (2, 1), (1, 2)):
            for h in range(2):
                make(snd.at[i % 2, k, h], land.at[i, k, h], rs_s.at[i, k, h], rs_r.at[i, k, h],
                     on_ctx(2 if d == 2 else 1)).wait_send()

    def rs_arrived(i):
        for h in range(2):
            arrived(land.at[i, 2, h], rs_r.at[i, 2, h], on_ctx(1))
            arrived(land.at[i, 1, h], rs_r.at[i, 1, h], on_ctx(2))

    def rs_rows(i, rw):
        parts = [keep[rw, pl.ds(h * half_w, half_w)] + land[i, 1, h, rw].astype(F32) + land[i, 2, h, rw].astype(F32)
                 for h in range(2)]
        return jnp.concatenate(parts, 1)

    def chunks(fn, init=0, size=CHUNK):
        return lax.fori_loop(0, t_rows // size, lambda i, v: fn(pl.ds(pl.multiple_of(i * size, size), size), v), init)

    sg = seg[...]
    start = jnp.zeros_like(sg)
    for doc in range(DOCS - 1):
        start = start + jnp.where(sg > doc, jnp.sum((sg == doc).astype(jnp.int32), -1, keepdims=True), 0)
    for b in range(n):
        start_s[b] = start[:, b * t_rows:(b + 1) * t_rows]

    for d in (1, 2, 3):
        arrived(packs.at[rel(d), f], pk_cr.at[rel(d)], on_ctx(d))
    for s in range(1, nf):
        f2 = (f + s) % nf
        send(packs.at[:, f], packs.at[:, f], pk_zs.at[s], pk_zr.at[f], on_z(f2))
    local_done(wq.at[:, c, f], loc.at[1])
    exchanged(0, wq)
    w_own(QKV)
    for s in range(1, nf):
        f2 = (f + s) % nf
        arrived(packs.at[:, f2], pk_zr.at[f2], on_z(f2))
    lane = lax.broadcasted_iota(jnp.int32, (8, 128), 1)
    per = 128 // rows
    for g in range(width // 128):
        acc = None
        for j in range(per):
            e = g * per + j
            piece = packs[e // nf, e % nf].astype(F32)[0:8]
            acc = piece if j == 0 else jnp.where(lane // rows == j, pltpu.roll(piece, j * rows, 1), acc)
        vecs[g] = acc
    for g in range(ffc // 128):
        acc = None
        for j in range(per):
            e = g * per + j
            k = e % 4
            piece = packs[c, e // 4].astype(F32)[8:16]
            piece = jnp.broadcast_to(piece[k:k + 1], (8, 128))
            acc = piece if j == 0 else jnp.where(lane // rows == j, pltpu.roll(piece, j * rows, 1), acc)
        inb[:, g * 128:(g + 1) * 128] = acc

    def vec(v):
        return jnp.concatenate([vecs[g, v:v + 1, :] for g in range(width // 128)], 1)

    def ln1(rw, _):
        z, _r = norm_parts(tok[rw].astype(F32))
        n1[c, rw] = (z * vec(0) + vec(1)).astype(BF16)
        return 0
    chunks(ln1)
    ag_start(0, n1)
    exchange(1, wi_hbm, wi, 1, ffc, half_f)
    local_done(cot.at[c], loc.at[0])
    ag_start(1, cot)
    local_done(wo.at[:, f], loc.at[2])
    for s in range(1, nf):
        w_step(QKV, s)
        if s == 1:
            w_own(OUT)
    ag_forward(0, n1)
    local_done(wi.at[:, c, f], loc.at[3])
    exchanged(1, wi)
    w_own(IN)
    for s in range(1, nf):
        w_step(OUT, s)
    ag_wait(0, n1, 1)
    ag_wait(0, n1, 3)
    w_arrived(QKV)

    def project(b, _):
        for p in range(2):
            pr = dot(n1[b], wq[p].reshape(width, 3 * pw), NN)
            qv = ((pr[:, :pw] + vecs[c * 2 + p, 2:3, :]).astype(BF16).astype(F32) * (HD ** -0.5)).astype(BF16)
            kv = pr[:, pw:2 * pw].astype(BF16)
            vv = (pr[:, 2 * pw:] + vecs[c * 2 + p, 3:4, :]).astype(BF16)
            kt, vt = kv.T, vv.T
            for e in range(2):
                q_s[2 * p + e, b] = qv[:, e * HD:(e + 1) * HD]
                k_s[2 * p + e, b] = kv[:, e * HD:(e + 1) * HD]
                v_s[2 * p + e, b] = vv[:, e * HD:(e + 1) * HD]
                kt_s[2 * p + e, b] = kt[e * HD:(e + 1) * HD]
                vt_s[2 * p + e, b] = vt[e * HD:(e + 1) * HD]
        return 0
    lax.fori_loop(0, n, project, 0)

    key_row = lax.broadcasted_iota(jnp.int32, (t_rows, t_rows), 0)
    query_col = lax.broadcasted_iota(jnp.int32, (t_rows, t_rows), 1)

    def scores(h, qb, kb, diagonal):
        s = dot(k_s[h, kb], q_s[h, qb], NT)
        ok = key_row >= start_s[qb] - kb * t_rows
        if diagonal:
            ok = ok & (key_row <= query_col)
        return jnp.where(ok, s, MASKED)

    def attend(h, qb):
        def step(kb, carry, diagonal=False):
            m, l, acc = carry
            s = scores(h, qb, kb, diagonal)
            m2 = jnp.maximum(m, jnp.max(s, 0, keepdims=True))
            p = jnp.exp(s - m2)
            a = jnp.exp(m - m2)
            return m2, l * a + jnp.sum(p, 0, keepdims=True), acc * a + dot(vt_s[h, kb], p.astype(BF16), NN)
        zero = jnp.zeros((1, t_rows), F32)
        carry = lax.fori_loop(0, qb, step, (zero + MASKED, zero, jnp.zeros((HD, t_rows), F32)))
        m, l, acc = step(qb, carry, True)
        att[qb, h] = (acc / l).astype(BF16)
        lse_s[h, qb] = m + jnp.log(l)

    for d in (3, 2, 1, 0):
        qb = rel(d)

        def heads(h, _):
            attend(h, qb)
            return 0
        lax.fori_loop(0, H // n, heads, 0)
        if d == 3:
            w_arrived(OUT)
            local_done(wb.at[:, f], loc.at[4])
            w_own(BACK)
        if 4 - d < nf:
            w_step(IN, 4 - d)
        for h in range(2):
            rs_put(0, d, h, dot(att[qb].reshape(hc, t_rows), wo[h].reshape(hc, half_w), TN))
    for s in range(5, nf):
        w_step(IN, s)
    ag_forward(1, cot)
    rs_arrived(0)

    def ln2(rw, _):
        res = tok[rw].astype(F32) + rs_rows(0, rw) + vec(4)
        resid[rw] = res
        z, _r = norm_parts(res)
        n2[c, rw] = (z * vec(5) + vec(6)).astype(BF16)
        return 0
    chunks(ln2)
    ag_start(2, n2)
    for s in range(1, nf):
        w_step(BACK, s)
    w_arrived(IN)
    ag_wait(1, cot, 1)
    ag_wait(1, cot, 3)
    w_arrived(BACK)

    ibg[...] = jnp.zeros_like(ibg)
    for d in (0, 1, 3, 2):
        b = rel(d)
        if d == 1:
            ag_wait(2, n2, 1)
        if d == 3:
            ag_forward(2, n2)
            ag_wait(2, n2, 3)

        def up(j, _):
            tmp1[...] = dot(n2[b], wi[j].reshape(width, half_f), NN)
            wide = jnp.concatenate([wb[h, pl.ds(j * (nf // 2), nf // 2)].reshape(half_f, half_w) for h in range(2)], 1)
            tmp2[...] = dot(cot[b], wide, NT)
            bias = inb[0:1, pl.ds(pl.multiple_of(j * half_f, half_f), half_f)]
            cols = pl.ds(pl.multiple_of(j * half_f, half_f), half_f)

            def one(rw, acc):
                a, da = gelu_both(tmp1[rw] + bias)
                act[b, rw, cols] = a.astype(BF16)
                gp = (tmp2[rw] * da).astype(BF16)
                gpre[b, rw, cols] = gp
                return acc + fold(gp.astype(F32))
            ibg[j] += chunks(one, jnp.zeros((8, half_f), F32))
            return 0
        lax.fori_loop(0, 2, up, 0)
        if d == 3:
            rs_sent(0)
        for h in range(2):
            wide = jnp.concatenate([wi[j, pl.ds(h * (n // 2), n // 2)].reshape(half_w, half_f) for j in range(2)], 1)
            rs_put(1, d, h, dot(gpre[b], wide, NT))

    grads = {QKV: (gwq, yq, zq), OUT: (gwo, yo, zo), IN: (gwi, yi, zi), BACK: (gwb, yb, zb)}
    alls = {QKV: aq, OUT: ao, IN: ai, BACK: ab}

    def g_y(kind):
        g, y, _z = grads[kind]
        send(g.at[1 - r], y, gy_s.at[kind], gy_r.at[kind], on_y)

    def g_z(kind):
        g, y, z = grads[kind]
        arrived(y, gy_r.at[kind], on_y)

        def add(i, _):
            g[r, i] = (g[r, i].astype(F32) + y[i].astype(F32)).astype(BF16)
            return 0
        lax.fori_loop(0, y.shape[0], add, 0)
        for s in range(1, nf):
            f2 = (f + s) % nf
            send(block(g, kind, r, f2), z.at[f], gz_s.at[kind, s], gz_r.at[kind, f], on_z(f2))

    def g_f(kind):
        g, _y, z = grads[kind]
        for s in range(1, nf):
            f2 = (f + s) % nf
            arrived(z.at[f2], gz_r.at[kind, f2], on_z(f2))
        if kind in (QKV, IN):
            fin, k = (fq, 0) if kind == QKV else (fi, 1)

            def add(i, _):
                tot = g[r, i, f].astype(F32)
                for s in range(1, nf):
                    tot = tot + z[(f + s) % nf, i].astype(F32)
                fin[i] = tot.astype(BF16)
                return 0
            lax.fori_loop(0, n, add, 0)
            for d in (2, 3, 1):
                send(fin.at[rel(d)], alls[kind].at[r, c], gc_s.at[k, d], gc_r.at[k, c], on_ctx(d))
            alls[kind][r, c] = fin[c]
        else:
            tot = g[r, f].astype(F32)
            for s in range(1, nf):
                tot = tot + z[(f + s) % nf].astype(F32)
            alls[kind][r] = tot.astype(BF16)
            send(alls[kind].at[r], alls[kind].at[r], gf_s.at[kind], gf_r.at[kind], on_y)

    def g_e(kind):
        k = 0 if kind == QKV else 1
        a = alls[kind]
        for d in (1, 2, 3):
            arrived(a.at[r, rel(d)], gc_r.at[k, rel(d)], on_ctx(d))
        send(a.at[r], a.at[r], gf_s.at[kind], gf_r.at[kind], on_y)

    def g_out(kind):
        a = alls[kind]
        arrived(a.at[1 - r], gf_r.at[kind], on_y)
        for h in range(2):
            if kind == OUT:
                go_o[:, h * half_w:(h + 1) * half_w] = ao[h].astype(F32)
            elif kind == BACK:
                gb_o[:, h * half_w:(h + 1) * half_w] = ab[h].astype(F32)
            else:
                for c2 in range(n):
                    if kind == IN:
                        gi_o[:, c2 * ffc + h * half_f:c2 * ffc + (h + 1) * half_f] = ai[h, c2].astype(F32)
                    else:
                        for j in range(3):
                            lo = j * width + c2 * hc + h * pw
                            gq_o[:, lo:lo + pw] = aq[h, c2, :, j * pw:(j + 1) * pw].astype(F32)

    def whole(buf, cols):
        v = buf[:, :, cols]
        return v.reshape(n * t_rows, v.shape[2])

    def grad_back(h):
        per_f = ffc // nf
        tiles = max(1, 256 // per_f)

        def one(i, _):
            a = whole(act, pl.ds(pl.multiple_of(i * 256, 256), 256))
            g = whole(cot, pl.ds(pl.multiple_of(h * half_w, half_w), half_w))
            v = dot(a, g, TN).astype(BF16)
            gwb[h, pl.ds(i * tiles, tiles)] = v.reshape(tiles, per_f, half_w)
            return 0
        lax.fori_loop(0, ffc // 256, one, 0)

    def grad_in(h):
        def one(i, _):
            a = whole(n2, pl.ds(pl.multiple_of(i * hc, hc), hc))
            g = whole(gpre, pl.ds(pl.multiple_of(h * half_f, half_f), half_f))
            gwi[h, i] = dot(a, g, TN).astype(BF16).reshape(nf, rows, half_f)
            return 0
        lax.fori_loop(0, n, one, 0)

    grad_back(1 - r)
    g_y(BACK)
    grad_back(r)
    rs_arrived(1)

    def ln2_back(rw, accs):
        gain, shift, bb, ob = accs
        g = rs_rows(1, rw)
        z, rstd = norm_parts(resid[rw])
        ct = cot[c, rw].astype(F32)
        gr = ct + norm_back(g, z, rstd, vec(5))
        gres[rw] = gr
        low = gr.astype(BF16)
        gbr[c, rw] = low
        return gain + fold(g * z), shift + fold(g), bb + fold(ct), ob + fold(low.astype(F32))
    zero8 = jnp.zeros((8, width), F32)
    accs = chunks(ln2_back, (zero8, zero8, zero8, zero8), 16)
    for i, a in zip((3, 4, 5, 2), accs):
        sums[i] = a
    ag_start(3, gbr)
    grad_in(1 - r)
    g_y(IN)
    grad_in(r)
    g_z(BACK)
    ag_forward(3, gbr)

    for d in (3, 2, 1, 0):
        for h in range(2):
            rs_put(2, d, h, dot(act[rel(d)], wb[h].reshape(ffc, half_w), NN))
    ag_wait(3, gbr, 1)
    ag_wait(3, gbr, 3)

    def g_attended(b, _):
        wide = jnp.concatenate([wo[h].reshape(hc, half_w) for h in range(2)], 1)
        g = dot(gbr[b], wide, NT).astype(BF16)
        gt = g.T.astype(F32).reshape(H // n, HD, t_rows)
        for h in range(H // n):
            do_s[h, b] = g[:, h * HD:(h + 1) * HD]
            delta_s[h, b] = jnp.sum(gt[h] * att[b, h].astype(F32), 0, keepdims=True)
        return 0
    lax.fori_loop(0, n, g_attended, 0)
    g_z(IN)

    def grad_out(h):
        tot = jnp.zeros((hc, half_w), F32)
        cols = pl.ds(pl.multiple_of(h * half_w, half_w), half_w)
        for b in range(n):
            tot = tot + dot(att[b].reshape(hc, t_rows), gbr[b, :, cols], NN)
        gwo[h] = tot.astype(BF16).reshape(nf, rows, half_w)
    grad_out(1 - r)
    g_y(OUT)
    grad_out(r)

    rs_arrived(2)

    def finish_out(rw, _):
        out_o[rw] = (resid[rw] + rs_rows(2, rw) + vec(7)).astype(BF16)
        return 0
    chunks(finish_out)

    def attend_back(h, e, p, qb):
        q, do = q_s[h, qb], do_s[h, qb]
        lse, delta = lse_s[h, qb], delta_s[h, qb]

        def step(kb, dqt, diagonal=False):
            pr = jnp.exp(scores(h, qb, kb, diagonal) - lse)
            dp = dot(v_s[h, kb], do, NT)
            ds = (pr * (dp - delta)).astype(BF16)
            dv_s[kb] += dot(pr.astype(BF16), do, NN)
            dk_s[kb] += dot(ds, q, NN)
            return dqt + dot(kt_s[h, kb], ds, NN)
        dqt = lax.fori_loop(0, qb, step, jnp.zeros((HD, t_rows), F32))
        dqt = step(qb, dqt, True) * (HD ** -0.5)
        gproj[p, qb, :, e * HD:(e + 1) * HD] = dqt.T.astype(BF16)

    def pair_back(p):
        for e in range(2):
            h = 2 * p + e
            dk_s[...] = jnp.zeros_like(dk_s)
            dv_s[...] = jnp.zeros_like(dv_s)

            def one(qb, _):
                attend_back(h, e, p, qb)
                return 0
            lax.fori_loop(0, n, one, 0)
            for b in range(n):
                gproj[p, b, :, pw + e * HD:pw + (e + 1) * HD] = dk_s[b].astype(BF16)
                gproj[p, b, :, 2 * pw + e * HD:2 * pw + (e + 1) * HD] = dv_s[b].astype(BF16)

        def grad_qkv(i, _):
            a = whole(n1, pl.ds(pl.multiple_of(i * hc, hc), hc))
            gwq[p, i] = dot(a, gproj[p].reshape(n * t_rows, 3 * pw), TN).astype(BF16).reshape(nf, rows, 3 * pw)
            return 0
        lax.fori_loop(0, n, grad_qkv, 0)

    pair_back(1 - r)
    g_y(QKV)
    g_f(BACK)
    g_z(OUT)
    pair_back(r)
    rs_sent(1)
    for d in (3, 2, 1, 0):
        for h in range(2):
            gp = jnp.concatenate([gproj[p, rel(d)] for p in range(2)], 1)
            wide = jnp.concatenate([wq[p, pl.ds(h * (n // 2), n // 2)].reshape(half_w, 3 * pw) for p in range(2)], 1)
            rs_put(3, d, h, dot(gp, wide, NT))
    g_z(QKV)
    g_f(IN)
    g_f(OUT)
    rs_arrived(3)

    def ln1_back(rw, accs):
        gain, shift = accs
        g = rs_rows(3, rw)
        z, rstd = norm_parts(tok[rw].astype(F32))
        gx_o[rw] = gres[rw] + norm_back(g, z, rstd, vec(0))
        return gain + fold(g * z), shift + fold(g)
    accs = chunks(ln1_back, (zero8, zero8), 16)
    sums[0], sums[1] = accs[0], accs[1]

    for i in range(8):
        row = jnp.sum(sums[i], 0, keepdims=True) if i < 6 else jnp.zeros((1, width), F32)
        for c2 in range(n):
            v6[c2, i:i + 1, :] = row[:, c2 * hc:(c2 + 1) * hc]
    for d in (1, 2, 3):
        send(v6.at[rel(d)], v6r.at[c], vc_s.at[d], vc_r.at[c], on_ctx(d))
    vs[...] = jnp.zeros_like(vs)
    for p in range(2):
        gsum = jnp.sum(gproj[p].reshape(n * t_rows, 3 * pw).astype(F32), 0, keepdims=True)
        v6[c, 6:7, p * pw:(p + 1) * pw] = gsum[:, :pw]
        v6[c, 7:8, p * pw:(p + 1) * pw] = gsum[:, 2 * pw:]
    for j in range(2):
        row = jnp.sum(ibg[j], 0, keepdims=True)
        for k in range(2):
            i = 8 + 2 * j + k
            vs[i:i + 1, :] = row[:, k * hc:(k + 1) * hc]
    for d in (1, 2, 3):
        arrived(v6r.at[rel(d)], vc_r.at[rel(d)], on_ctx(d))
    vs[0:8] = v6[c] + v6r[rel(1)] + v6r[rel(2)] + v6r[rel(3)]
    send(vs, vy, vy_s.at[0], vy_r.at[0], on_y)
    g_e(IN)
    g_f(QKV)
    arrived(vy, vy_r.at[0], on_y)
    vs2[...] = vs[...] + vy[...]
    for s in range(1, nf):
        send(vs2, vz.at[f], vz_s.at[s], vz_r.at[f], on_z((f + s) % nf))
    g_e(QKV)
    g_out(BACK)
    g_out(OUT)
    g_out(IN)
    tot = vs2[...]
    for s in range(1, nf):
        f2 = (f + s) % nf
        arrived(vz.at[f2], vz_r.at[f2], on_z(f2))
        tot = tot + vz[f2]
    gv_o[...] = tot
    g_out(QKV)
    rs_sent(2)
    rs_sent(3)
    for end in ends:
        end()


def shards(n, nf, tokens, segments, ln1_gain, ln1_bias, w_qkv, q_bias, v_bias, w_out, out_bias,
           ln2_gain, ln2_bias, w_in, in_bias, w_back, back_bias, cotangent):
    t_rows, width = tokens.shape[1], tokens.shape[2]
    rows, brows = w_qkv.shape[0], w_back.shape[0]
    ffc = w_in.shape[1] // n
    slots = segments.shape[1]
    heads = H // n
    hc, half_w, half_f = width // n, width // 2, ffc // 2
    q3 = 3 * hc // 2
    small = jnp.stack([ln1_gain, ln1_bias, q_bias, v_bias, out_bias, ln2_gain, ln2_bias, back_bias])
    small = jnp.concatenate([small, in_bias.reshape(4, rows), jnp.zeros((4, rows), BF16)], 0)
    small = jnp.pad(small, ((0, 0), (0, 128 - rows)))
    dims = (n, nf, t_rows, width, rows, brows, ffc)
    vm = pltpu.VMEM
    dma = pltpu.SemaphoreType.DMA
    per_head = (heads, n, t_rows, HD)
    per_head_t = (heads, n, HD, t_rows)
    scratch = [
        vm((2, n, nf, rows, q3), BF16), vm((2, nf, rows, half_w), BF16), vm((2, n, nf, rows, half_f), BF16),
        vm((2, nf, brows, half_w), BF16), vm((n, nf, 16, 128), BF16), vm((width // 128, 8, 128), F32), vm((8, ffc), F32),
        vm((n, t_rows, width), BF16), vm((n, t_rows, width), BF16), vm((n, t_rows, width), BF16), vm((n, t_rows, width), BF16),
        vm(per_head, BF16), vm(per_head, BF16), vm(per_head, BF16), vm(per_head, BF16), vm(per_head_t, BF16), vm(per_head_t, BF16),
        vm((n, heads, HD, t_rows), BF16), vm((n, t_rows, ffc), BF16), vm((n, t_rows, ffc), BF16), vm((2, n, t_rows, q3), BF16),
        vm((n, 1, t_rows), jnp.int32), vm((heads, n, 1, t_rows), F32), vm((heads, n, 1, t_rows), F32),
        vm((t_rows, width), F32), vm((t_rows, width), F32), vm((t_rows, width), F32), vm((t_rows, half_f), F32), vm((t_rows, half_f), F32),
        vm((2, 3, 2, t_rows, half_w), BF16), vm((4, 3, 2, t_rows, half_w), BF16),
        vm((n, t_rows, HD), F32), vm((n, t_rows, HD), F32),
        vm((2, n, nf, rows, q3), BF16), vm((2, nf, rows, half_w), BF16), vm((2, n, nf, rows, half_f), BF16), vm((2, nf, brows, half_w), BF16),
        vm((n, nf, rows, q3), BF16), vm((nf, rows, half_w), BF16), vm((n, nf, rows, half_f), BF16), vm((nf, brows, half_w), BF16),
        vm((nf, n, rows, q3), BF16), vm((nf, rows, half_w), BF16), vm((nf, n, rows, half_f), BF16), vm((nf, brows, half_w), BF16),
        vm((n, rows, q3), BF16), vm((n, rows, half_f), BF16),
        vm((2, n, rows, q3), BF16), vm((2, rows, half_w), BF16), vm((2, n, rows, half_f), BF16), vm((2, brows, half_w), BF16),
        vm((n, 8, hc), F32), vm((n, 8, hc), F32), vm((16, hc), F32), vm((16, hc), F32), vm((16, hc), F32), vm((nf, 16, hc), F32),
        vm((2, 8, half_f), F32), vm((8, 8, width), F32),
        dma((5,)), dma((4,)), dma((n,)), dma((nf,)), dma((nf,)), dma((2, 4)), dma((2, n)),
        dma((4, 2, nf)), dma((4, nf)), dma((4, nf)), dma((4, nf)), dma((4, 3)), dma((4, n)), dma((4, 3, 2)), dma((4, 3, 2)),
        dma((4,)), dma((4,)), dma((4, nf)), dma((4, nf)), dma((2, 4)), dma((2, n)), dma((4,)), dma((4,)),
        dma((4,)), dma((n,)), dma((1,)), dma((1,)), dma((nf,)), dma((nf,)),
    ]
    shape = jax.ShapeDtypeStruct
    in_vmem, in_hbm = pl.BlockSpec(memory_space=vm), pl.BlockSpec(memory_space=pl.ANY)
    outs = pl.pallas_call(
        functools.partial(body, dims),
        out_shape=[shape((t_rows, width), BF16), shape((t_rows, width), F32), shape(w_qkv.shape, F32), shape(w_out.shape, F32),
                   shape(w_in.shape, F32), shape(w_back.shape, F32), shape((16, hc), F32)],
        in_specs=[in_vmem, in_hbm, in_vmem, in_vmem] + [in_hbm] * 4,
        out_specs=[in_vmem] * 7,
        scratch_shapes=scratch,
        compiler_params=pltpu.CompilerParams(collective_id=0, has_side_effects=True, vmem_limit_bytes=67043328),
    )(tokens[0], cotangent[0], segments, small, w_qkv, w_out, w_in, w_back)
    layer_output, input_grad, g_qkv, g_out, g_in, g_back, gv = outs
    f = lax.axis_index("fsdp")
    mine = lax.dynamic_slice_in_dim(gv[:8], f * rows, rows, 1)
    g_in_bias = lax.dynamic_slice_in_dim(gv[8:12].reshape(-1), f * 4 * rows, 4 * rows, 0)
    return (layer_output[None], input_grad[None], mine[0], mine[1], g_qkv, mine[6], mine[7], g_out,
            mine[2], mine[3], mine[4], g_in, g_in_bias, g_back, mine[5])


def solution(mesh):
    both = ("ctx", "fsdp")
    own, rows = P(both), P(both, None)
    seqs = P(("fsdp", "rep"), "ctx", None)
    in_specs = (seqs, P(("fsdp", "rep"), None), own, own, rows, own, own, rows, own, own, own, rows, own, rows, own, seqs)
    out_specs = (seqs, seqs, own, own, rows, own, own, rows, own, own, own, rows, own, rows, own)
    run = functools.partial(shards, mesh.shape["ctx"], mesh.shape["fsdp"])
    return jax.shard_map(run, mesh=mesh, in_specs=in_specs, out_specs=out_specs, check_vma=False)
```

time: 707 us -> 236 us (0.33); the launches traced: 695 us -> 231 us
  waiting for transfers between devices: 425 us -> 0 us
  Pallas kernels: 0 us -> 218 us
  matrix products: 106 us -> 0 us
  blocking collectives: 80 us -> 0 us
  other arithmetic: 32.6 us -> 0 us
  starting transfers between devices: 18.3 us -> 0 us
  between operations: 15.5 us -> 0.74 us
    pallas_call x0 -> x1, Pallas kernels: none -> 218 us  [shards(): pl.pallas_call(functools.partial(body, dims), out_shape=[shape((t_rows, w...]
    reduce_scatter x8 -> x0, waiting for transfers between devices: 170 us -> none  [the longest x4 103 us: ctx_scatter(): lax.psum_scatter(x.astype(BF16), 'ctx', scatter_dimension=0, tiled=True)]
    all_gather x7 -> x0, waiting for transfers between devices: 147 us -> none  [the longest x4 74.5 us: ctx_gather(): return lax.all_gather(x, 'ctx', axis=0, tiled=True)]
    dot_general x17 -> x0, matrix products: 96.3 us -> none  [the longest x12 60.8 us: dot(): return lax.dot_general(a, b, (dims, ((), ())), preferred_element_type=F32)]
    unnamed x18 -> x0, waiting for transfers between devices: 50.2 us -> none
    psum x1 -> x0, waiting for transfers between devices: 49.9 us -> none  [shards(): grads = [lax.psum(g, 'rep').astype(F32) for g in grads]]
    all_gather x3 -> x0, blocking collectives: 47.9 us -> none  [the longest x1 29.2 us: shards(): small = lax.all_gather(small, OWN, axis=1, tiled=True).astype(F32)]
    all_to_all x2 -> x0, blocking collectives: 20.1 us -> none  [the longest x1 10.5 us: shards(): wi = lax.all_to_all(w_in.reshape(rows_in, n, ffc), 'ctx', 1, 0)]
  transfers between devices with their start and end apart: 19 -> 0, of which waited for: 16 -> 0; matrix products, arithmetic and copies ran while one was open for 15% -> 0% of each run, Pallas kernels for 0% -> 0%
where the time goes in v2:
time: 236 us; the launch traced here: 231 us
  Pallas kernels  218 us (92%)
  local copies, waits for them, and re-layouts  12.6 us (5%)
    pallas_call x1, Pallas kernels, shards(): pl.pallas_call(functools.partial(body, dims), out_shape=[shape((t_rows, w...  218 us
    unnamed x36, local copies, waits for them, and re-layouts  9.82 us

profile of v2, /device:TPU:29, one launch (start us, length us, event | category | flops | bytes accessed | tf_op | source)
XLA Modules:
  0.0 231.3 jit_solution(7166485320946758435)
XLA Ops:
  0.7 0.0 copy-start.13
  0.7 0.6 copy-done.13
  1.3 0.1 reshape.36
  1.4 0.0 copy-start.12
  1.4 0.0 copy-start.8
  1.4 0.0 copy-start.9
  1.4 0.0 copy-start.10
  1.4 0.0 copy-start.11
  1.4 0.0 copy-start.5
  1.4 0.0 copy-start.6
  1.4 0.0 copy-start.7
  1.5 0.6 copy-done.12
  2.0 0.0 copy-done.8
  2.1 0.0 copy-done.9
  2.1 0.0 copy-done.10
  2.1 0.0 copy-done.11
  2.1 0.0 copy-done.5
  2.1 0.0 copy-done.6
  2.1 0.0 copy-done.7
  2.2 0.1 concatenate.3
  2.2 0.6 pad.4.pack
  2.8 218.0 %shard_map.271 = (bf16[256,1024]{1,0:T(8,128)(2,1)}, f32[256,1024]{1,0:T(8,128)}, f32[64,3072]{1,0:T(8,128)}, f32[64,1024]{1,0:T(8,128)}, f32[64,4096]{1,0:T(8,1...) custom-call(bf16[256,1024]{1,0:T(8,128)(2,1)} %bitcast.32, bf16[256,1024]{1,0:T(8,128)(2,1)} %bitcast.33, s32[1,1024]{1,0:T(1,128)} %seg.1, ...), custom_call_target="tpu_custom_call" | custom-call | tf_op jit(solution)/shard_map/pallas_call | solution.py:680
  220.8 0.0 copy-start.2
  220.8 0.8 slice.30
  221.6 0.1 constant_dynamic-slice_fusion
  221.7 0.5 slice_bitcast_fusion.1
  222.2 0.7 slice_bitcast_fusion
  222.9 0.6 dynamic_slice.7
  223.6 1.9 copy.38
  225.4 0.0 copy-done.2
  225.4 0.0 copy-start.3
  225.5 1.0 copy.39
  226.4 0.5 copy-done.3
  227.0 0.0 copy-start.4
  227.0 0.0 copy-start.1
  227.0 0.9 copy.40
  227.8 0.2 copy-done.4
  228.1 0.7 copy.41
  228.8 0.0 copy-done.1
  228.8 0.0 copy-start
  228.8 1.0 copy.42
  229.7 0.6 copy-done
  230.4 1.0 copy.43
  (2 shorter events, 0.0 us)
Async XLA Ops:
  0.7 0.7 copy-start.13
  1.4 0.7 copy-start.12
  1.4 0.7 copy-start.8
  1.4 0.7 copy-start.9
  1.4 0.7 copy-start.10
  1.4 0.7 copy-start.11
  1.4 0.7 copy-start.5
  1.4 0.7 copy-start.6
  1.4 0.7 copy-start.7
  220.8 4.6 %copy-start.2 = (f32[256,1024]{1,0:T(8,128)S(1)}, f32[256,1024]{1,0:T(8,128)}, u32[]{:S(2)}) copy-start(f32[256,1024]{1,0:T(8,128)} %get-tuple-element.23) | copy-start | bytes 3145732
  225.4 1.5 copy-start.3
  227.0 1.1 copy-start.4
  227.0 1.8 copy-start.1
  228.8 1.6 copy-start

commit v3 on v2

--- a/solution.py
+++ b/solution.py
@@ -55,7 +55,7 @@
          dk_s, dv_s, gwq, gwo, gwi, gwb, yq, yo, yi, yb, zq, zo, zi, zb, fq, fi, aq, ao, ai, ab,
          v6, v6r, vs, vy, vs2, vz, ibg, sums,
          loc, pk_cs, pk_cr, pk_zs, pk_zr, wc_s, wc_r, wz_s, wz_r, wy_s, wy_r, ag_s, ag_r, rs_s, rs_r,
-         gy_s, gy_r, gz_s, gz_r, gc_s, gc_r, gf_s, gf_r, vc_s, vc_r, vy_s, vy_r, vz_s, vz_r):
+         gy_s, gy_r, gz_s, gz_r, gc_s, gc_r, gf_s, gf_r, vc_s, vc_r, vy_s, vy_r, vz_s, vz_r, out_s):
     n, nf, t_rows, width, rows, brows, ffc = dims
     half_w, half_f = width // 2, ffc // 2
     hc = width // n
@@ -103,14 +103,15 @@
     def local_done(dst, sem):
         pltpu.make_async_copy(dst, dst, sem).wait()
 
-    local(cot_in, cot.at[c], loc.at[0])
     for h in range(2):
         for j in range(3):
             local(wq_hbm.at[:, pl.ds(pl.multiple_of(j * width + c * hc + h * pw, pw), pw)],
                   wq.at[h, c, f, :, pl.ds(j * pw, pw)], loc.at[1])
         local(wo_hbm.at[:, pl.ds(h * half_w, half_w)], wo.at[h, f], loc.at[2])
+        local(wb_hbm.at[:, pl.ds(h * half_w, half_w)], wb.at[h, f], loc.at[4])
+    for h in range(2):
         local(wi_hbm.at[:, pl.ds(pl.multiple_of(c * ffc + h * half_f, half_f), half_f)], wi.at[h, c, f], loc.at[3])
-        local(wb_hbm.at[:, pl.ds(h * half_w, half_w)], wb.at[h, f], loc.at[4])
+    local(cot_in, cot.at[c], loc.at[0])
     packs[c, f] = pack[...]
     barrier = pltpu.get_barrier_semaphore()
     peers = [on_ctx(d) for d in (1, 2, 3)] + [on_z((f + s) % nf) for s in range(1, nf)] + [on_y]
@@ -136,37 +137,60 @@
             arrived(buf.at[:, rel(d), f], wc_r.at[kind, rel(d)], on_ctx(d))
 
     exchange(0, wq_hbm, wq, 3, hc, pw)
+    exchange(1, wi_hbm, wi, 1, ffc, half_f)
 
     bufs = {QKV: wq, OUT: wo, IN: wi, BACK: wb}
 
     def block(buf, kind, h, f2):
         return buf.at[h, :, f2] if kind in (QKV, IN) else buf.at[h, f2]
 
-    def w_send(kind, way, src, cond):
-        nxt = f + 1 if way == 0 else f - 1
-        b = block(bufs[kind], kind, r, src)
-        send(b, b, wz_s.at[kind, way, src], wz_r.at[kind, src], on_z(nxt), cond)
-
-    def w_own(kind):
-        w_send(kind, 0, f, f + 1 < nf)
-        w_send(kind, 1, f, f >= 1)
-
-    def w_step(kind, s):
-        for way in range(2):
-            src = f - s if way == 0 else f + s
-            ok = src >= 0 if way == 0 else src < nf
-            b = block(bufs[kind], kind, r, src)
+    pieces = {QKV: 2, OUT: 1, IN: 2, BACK: 2}
+
+    def part(kind, h, f2, p):
+        buf = bufs[kind]
+        if kind in (QKV, IN):
+            return buf.at[h, pl.ds(p * (n // 2), n // 2), f2]
+        return buf.at[h, f2] if kind == OUT else buf.at[h, f2, pl.ds(p * (brows // 2), brows // 2)]
+
+    def w_z(kind, p, slot, src, dst, cond):
+        b = part(kind, r, src, p)
+        send(b, b, wz_s.at[kind, p, slot], wz_r.at[kind, p, src], on_z(dst), cond)
+
+    def w_own(kind, p):
+        for k, s in enumerate([1] + list(range(3, nf))):
+            w_z(kind, p, 2 + 2 * k, f, f + s, f + s < nf)
+            w_z(kind, p, 3 + 2 * k, f, f - s, f >= s)
+
+    def sources(s):
+        return (f - s, f >= s), (f + s, f + s < nf)
+
+    def w_relay(kind, p):
+        for way, (src, ok) in enumerate(sources(1)):
+            w_z(kind, p, way, src, 2 * f - src, ok & ((f + 1 < nf) if way == 0 else (f >= 1)))
+
+    def w_swap(kind, p, s):
+        for src, ok in sources(s):
+            b = part(kind, r, src, p)
 
             @pl.when(ok)
             def _():
-                arrived(b, wz_r.at[kind, src], on_y)
-            w_send(kind, way, src, ok & ((f + 1 < nf) if way == 0 else (f >= 1)))
-            send(b, b, wy_s.at[kind, src], wy_r.at[kind, src], on_y, ok)
+                arrived(b, wz_r.at[kind, p, src], on_y)
+            send(b, b, wy_s.at[kind, p, src], wy_r.at[kind, p, src], on_y, ok)
+
+    def w_step(kind, p, s):
+        if s == 3:
+            for far in range(3, nf):
+                w_swap(kind, p, far)
+        elif s < nf:
+            w_swap(kind, p, s)
+            if s == 1:
+                w_relay(kind, p)
 
     def w_arrived(kind):
-        for s in range(1, nf):
-            f2 = (f + s) % nf
-            arrived(block(bufs[kind], kind, 1 - r, f2), wy_r.at[kind, f2], on_y)
+        for p in range(pieces[kind]):
+            for s in range(1, nf):
+                f2 = (f + s) % nf
+                arrived(part(kind, 1 - r, f2, p), wy_r.at[kind, p, f2], on_y)
 
     def ag_start(i, buf):
         for d, k in ((2, 0), (1, 1)):
@@ -218,6 +242,10 @@
     for b in range(n):
         start_s[b] = start[:, b * t_rows:(b + 1) * t_rows]
 
+    local_done(wo.at[:, f], loc.at[2])
+    w_own(OUT, 0)
+    local_done(wb.at[:, f], loc.at[4])
+    w_own(BACK, 0)
     for d in (1, 2, 3):
         arrived(packs.at[rel(d), f], pk_cr.at[rel(d)], on_ctx(d))
     for s in range(1, nf):
@@ -225,7 +253,10 @@
         send(packs.at[:, f], packs.at[:, f], pk_zs.at[s], pk_zr.at[f], on_z(f2))
     local_done(wq.at[:, c, f], loc.at[1])
     exchanged(0, wq)
-    w_own(QKV)
+    w_own(QKV, 0)
+    w_own(QKV, 1)
+    w_swap(OUT, 0, 1)
+    w_swap(BACK, 0, 1)
     for s in range(1, nf):
         f2 = (f + s) % nf
         arrived(packs.at[:, f2], pk_zr.at[f2], on_z(f2))
@@ -257,20 +288,23 @@
         return 0
     chunks(ln1)
     ag_start(0, n1)
-    exchange(1, wi_hbm, wi, 1, ffc, half_f)
     local_done(cot.at[c], loc.at[0])
     ag_start(1, cot)
-    local_done(wo.at[:, f], loc.at[2])
-    for s in range(1, nf):
-        w_step(QKV, s)
-        if s == 1:
-            w_own(OUT)
-    ag_forward(0, n1)
+    w_step(QKV, 0, 1)
+    w_step(QKV, 1, 1)
+    w_relay(OUT, 0)
     local_done(wi.at[:, c, f], loc.at[3])
     exchanged(1, wi)
-    w_own(IN)
-    for s in range(1, nf):
-        w_step(OUT, s)
+    w_own(IN, 0)
+    w_own(IN, 1)
+    w_relay(BACK, 0)
+    w_own(BACK, 1)
+    for s in (3, 2):
+        w_step(QKV, 0, s)
+        w_step(QKV, 1, s)
+    w_step(OUT, 0, 3)
+    w_step(OUT, 0, 2)
+    ag_forward(0, n1)
     ag_wait(0, n1, 1)
     ag_wait(0, n1, 3)
     w_arrived(QKV)
@@ -315,24 +349,23 @@
         att[qb, h] = (acc / l).astype(BF16)
         lse_s[h, qb] = m + jnp.log(l)
 
+    polls = [[(IN, 0, 1), (IN, 0, 3)], [(BACK, 0, 3), (BACK, 0, 2)], [(IN, 1, 1), (IN, 1, 3)], [], [(BACK, 1, 1)], [(BACK, 1, 3)],
+             [(IN, 0, 2)], [(IN, 1, 2)]]
     for d in (3, 2, 1, 0):
         qb = rel(d)
-
-        def heads(h, _):
-            attend(h, qb)
-            return 0
-        lax.fori_loop(0, H // n, heads, 0)
+        for k in range(2):
+            def heads(h, _):
+                attend(h, qb)
+                return 0
+            lax.fori_loop(k * (H // n // 2), (k + 1) * (H // n // 2), heads, 0)
+            for poll in polls[2 * (3 - d) + k]:
+                w_step(*poll)
         if d == 3:
             w_arrived(OUT)
-            local_done(wb.at[:, f], loc.at[4])
-            w_own(BACK)
-        if 4 - d < nf:
-            w_step(IN, 4 - d)
+        if d == 2:
+            ag_forward(1, cot)
         for h in range(2):
             rs_put(0, d, h, dot(att[qb].reshape(hc, t_rows), wo[h].reshape(hc, half_w), TN))
-    for s in range(5, nf):
-        w_step(IN, s)
-    ag_forward(1, cot)
     rs_arrived(0)
 
     def ln2(rw, _):
@@ -343,8 +376,7 @@
         return 0
     chunks(ln2)
     ag_start(2, n2)
-    for s in range(1, nf):
-        w_step(BACK, s)
+    w_step(BACK, 1, 2)
     w_arrived(IN)
     ag_wait(1, cot, 1)
     ag_wait(1, cot, 3)
@@ -432,22 +464,20 @@
             arrived(a.at[r, rel(d)], gc_r.at[k, rel(d)], on_ctx(d))
         send(a.at[r], a.at[r], gf_s.at[kind], gf_r.at[kind], on_y)
 
+    outs = {QKV: gq_o, OUT: go_o, IN: gi_o, BACK: gb_o}
+
     def g_out(kind):
-        a = alls[kind]
+        a, o = alls[kind], outs[kind]
         arrived(a.at[1 - r], gf_r.at[kind], on_y)
         for h in range(2):
-            if kind == OUT:
-                go_o[:, h * half_w:(h + 1) * half_w] = ao[h].astype(F32)
-            elif kind == BACK:
-                gb_o[:, h * half_w:(h + 1) * half_w] = ab[h].astype(F32)
-            else:
-                for c2 in range(n):
-                    if kind == IN:
-                        gi_o[:, c2 * ffc + h * half_f:c2 * ffc + (h + 1) * half_f] = ai[h, c2].astype(F32)
-                    else:
-                        for j in range(3):
-                            lo = j * width + c2 * hc + h * pw
-                            gq_o[:, lo:lo + pw] = aq[h, c2, :, j * pw:(j + 1) * pw].astype(F32)
+            if kind in (OUT, BACK):
+                local(a.at[h], o.at[:, pl.ds(h * half_w, half_w)], out_s.at[kind])
+                continue
+            for c2 in range(n):
+                for j in range(3 if kind == QKV else 1):
+                    w = pw if kind == QKV else half_f
+                    lo = j * width + c2 * hc + h * pw if kind == QKV else c2 * ffc + h * half_f
+                    local(a.at[h, c2, :, pl.ds(j * w, w)], o.at[:, pl.ds(lo, w)], out_s.at[kind])
 
     def whole(buf, cols):
         v = buf[:, :, cols]
@@ -628,12 +658,35 @@
         f2 = (f + s) % nf
         arrived(vz.at[f2], vz_r.at[f2], on_z(f2))
         tot = tot + vz[f2]
-    gv_o[...] = tot
+    mine, mine_in = tot[:, :rows], tot[8:9, :4 * rows]
+    for f2 in range(1, nf):
+        row, lo = 8 + f2 * 4 * rows // hc, f2 * 4 * rows % hc
+        mine = jnp.where(f == f2, tot[:, f2 * rows:(f2 + 1) * rows], mine)
+        mine_in = jnp.where(f == f2, tot[row:row + 1, lo:lo + 4 * rows], mine_in)
+    gv_o[0:16, :rows] = mine
+    gv_o[16:17, :4 * rows] = mine_in
     g_out(QKV)
     rs_sent(2)
     rs_sent(3)
     for end in ends:
         end()
+    for kind in range(4):
+        local_done(alls[kind], out_s.at[kind])
+
+
+def finish(lo_i, gx_i, gq_i, go_i, gi_i, gb_i, lo_o, gx_o, gq_o, go_o, gi_o, gb_o,
+           lo_b, gx_b, gq_b, go_b, gi_b, gb_b, gq_w, go_w, gi_w, gb_w, sem_i, sem_o):
+    parts = [(gb_i, gb_b, gb_w, gb_o), (gi_i, gi_b, gi_w, gi_o), (gq_i, gq_b, gq_w, gq_o), (go_i, go_b, go_w, go_o),
+             (gx_i, gx_b, gx_b, gx_o), (lo_i, lo_b, lo_b, lo_o)]
+    for k, (src, low, wide, dst) in enumerate(parts):
+        pltpu.make_async_copy(src, low, sem_i.at[k]).start()
+    for k, (src, low, wide, dst) in enumerate(parts):
+        pltpu.make_async_copy(src, low, sem_i.at[k]).wait()
+        if wide is not low:
+            wide[...] = low[...].astype(F32)
+        pltpu.make_async_copy(wide, dst, sem_o.at[k]).start()
+    for k, (src, low, wide, dst) in enumerate(parts):
+        pltpu.make_async_copy(wide, dst, sem_o.at[k]).wait()
 
 
 def shards(n, nf, tokens, segments, ln1_gain, ln1_bias, w_qkv, q_bias, v_bias, w_out, out_bias,
@@ -671,27 +724,34 @@
         vm((n, 8, hc), F32), vm((n, 8, hc), F32), vm((16, hc), F32), vm((16, hc), F32), vm((16, hc), F32), vm((nf, 16, hc), F32),
         vm((2, 8, half_f), F32), vm((8, 8, width), F32),
         dma((5,)), dma((4,)), dma((n,)), dma((nf,)), dma((nf,)), dma((2, 4)), dma((2, n)),
-        dma((4, 2, nf)), dma((4, nf)), dma((4, nf)), dma((4, nf)), dma((4, 3)), dma((4, n)), dma((4, 3, 2)), dma((4, 3, 2)),
+        dma((4, 2, 4 + 2 * max(0, nf - 3))), dma((4, 2, nf)), dma((4, 2, nf)), dma((4, 2, nf)), dma((4, 3)), dma((4, n)), dma((4, 3, 2)), dma((4, 3, 2)),
         dma((4,)), dma((4,)), dma((4, nf)), dma((4, nf)), dma((2, 4)), dma((2, n)), dma((4,)), dma((4,)),
-        dma((4,)), dma((n,)), dma((1,)), dma((1,)), dma((nf,)), dma((nf,)),
+        dma((4,)), dma((n,)), dma((1,)), dma((1,)), dma((nf,)), dma((nf,)), dma((4,)),
     ]
     shape = jax.ShapeDtypeStruct
     in_vmem, in_hbm = pl.BlockSpec(memory_space=vm), pl.BlockSpec(memory_space=pl.ANY)
     outs = pl.pallas_call(
         functools.partial(body, dims),
-        out_shape=[shape((t_rows, width), BF16), shape((t_rows, width), F32), shape(w_qkv.shape, F32), shape(w_out.shape, F32),
-                   shape(w_in.shape, F32), shape(w_back.shape, F32), shape((16, hc), F32)],
+        out_shape=[shape((t_rows, width), BF16), shape((t_rows, width), F32), shape(w_qkv.shape, BF16), shape(w_out.shape, BF16),
+                   shape(w_in.shape, BF16), shape(w_back.shape, BF16), shape((24, hc), F32)],
         in_specs=[in_vmem, in_hbm, in_vmem, in_vmem] + [in_hbm] * 4,
-        out_specs=[in_vmem] * 7,
+        out_specs=[in_vmem] * 2 + [in_hbm] * 4 + [in_vmem],
         scratch_shapes=scratch,
         compiler_params=pltpu.CompilerParams(collective_id=0, has_side_effects=True, vmem_limit_bytes=67043328),
     )(tokens[0], cotangent[0], segments, small, w_qkv, w_out, w_in, w_back)
-    layer_output, input_grad, g_qkv, g_out, g_in, g_back, gv = outs
-    f = lax.axis_index("fsdp")
-    mine = lax.dynamic_slice_in_dim(gv[:8], f * rows, rows, 1)
-    g_in_bias = lax.dynamic_slice_in_dim(gv[8:12].reshape(-1), f * 4 * rows, 4 * rows, 0)
+    gv = outs[6]
+    grads = [w_qkv, w_out, w_in, w_back]
+    layer_output, input_grad, g_qkv, g_out, g_in, g_back = pl.pallas_call(
+        finish,
+        out_shape=[shape((t_rows, width), BF16), shape((t_rows, width), F32)] + [shape(g.shape, F32) for g in grads],
+        in_specs=[in_hbm] * 6,
+        out_specs=[in_hbm] * 6,
+        scratch_shapes=[vm((t_rows, width), BF16), vm((t_rows, width), F32)] + [vm(g.shape, BF16) for g in grads]
+        + [vm(g.shape, F32) for g in grads] + [dma((6,)), dma((6,))],
+    )(*outs[:6])
+    mine = gv[:8, :rows]
     return (layer_output[None], input_grad[None], mine[0], mine[1], g_qkv, mine[6], mine[7], g_out,
-            mine[2], mine[3], mine[4], g_in, g_in_bias, g_back, mine[5])
+            mine[2], mine[3], mine[4], g_in, gv[16, :4 * rows], g_back, mine[5])
 
 
 def solution(mesh):

time: 236 us -> 213 us (0.903)
  Pallas kernels: 218 us -> 204 us
  local copies, waits for them, and re-layouts: 12.6 us -> 4.84 us
    pallas_call x1, Pallas kernels: 218 us -> 201 us  [shards(): pl.pallas_call(functools.partial(body, dims), out_shape=[shape((t_rows, w...]
    unnamed x36 -> x18, local copies, waits for them, and re-layouts: 9.82 us -> 1.32 us
    pallas_call x0 -> x1, Pallas kernels: none -> 3.39 us  [shards(): pl.pallas_call(finish, out_shape=[shape((t_rows, width), BF16), shape((t_...]
where the time goes in v3:
time: 213 us; the launch traced here: 210 us
  Pallas kernels  204 us (96%)
  local copies, waits for them, and re-layouts  4.84 us (2%)
    pallas_call x1, Pallas kernels, shards(): pl.pallas_call(functools.partial(body, dims), out_shape=[shape((t_rows, w...  201 us

profile of v3, /device:TPU:29, one launch (start us, length us, event | category | flops | bytes accessed | tf_op | source)
XLA Modules:
  0.0 210.0 jit_solution(15700712406789222447)
XLA Ops:
  0.6 0.0 copy-start.8
  0.7 0.0 copy-start.7
  0.7 0.6 copy-done.8
  1.3 0.0 copy-start.3
  1.3 0.0 copy-start.4
  1.3 0.0 copy-start.5
  1.3 0.0 copy-start.6
  1.3 0.1 reshape.33
  1.4 0.0 copy-start
  1.4 0.0 copy-start.1
  1.4 0.0 copy-start.2
  1.4 0.0 copy-done.7
  1.4 0.5 copy-done.3
  2.0 0.0 copy-done.4
  2.0 0.0 copy-done.5
  2.0 0.0 copy-done.6
  2.0 0.0 copy-done
  2.1 0.0 copy-done.1
  2.1 0.0 copy-done.2
  2.1 0.1 concatenate.3
  2.1 0.6 pad.4.pack
  2.8 200.9 %shard_map.271 = (bf16[256,1024]{1,0:T(8,128)(2,1)}, f32[256,1024]{1,0:T(8,128)}, bf16[64,3072]{1,0:T(8,128)(2,1)}, bf16[64,1024]{1,0:T(8,128)(2,1)}, bf16[64,40...) custom-call(bf16[256,1024]{1,0:T(8,128)(2,1)} %bitcast.29, bf16[256,1024]{1,0:T(8,128)(2,1)} %bitcast.30, ...), custom_call_target="tpu_custom_call" | custom-call | tf_op jit(solution)/shard_map/pallas_call | solution.py:733
  203.7 1.3 slice.43
  205.0 1.5 slice_bitcast_fusion
  206.5 3.4 %shard_map.272 = (bf16[256,1024]{1,0:T(8,128)(2,1)}, f32[256,1024]{1,0:T(8,128)}, f32[64,3072]{1,0:T(8,128)}, f32[64,1024]{1,0:T(8,128)}, f32[64,4096]{1,0:T(8,128)}, /*index=5*/f32[256,1024]{1,0:T(8,128)}) custom-call(bf16[256,1024]{1,0:T(8,128)(2,1)} %get-tuple-element.28.lo_i, f32[256,1024]{1,0:T(8,128)} %get-tuple-element.29.gx_i, ...), custom_call_target="tpu_custom_call" | custom-call | tf_op jit(solution)/shard_map/pallas_call | solution.py:744
  (1 shorter events, 0.0 us)
Async XLA Ops:
  0.6 0.7 copy-start.8
  0.7 0.8 copy-start.7
  1.3 0.7 copy-start.3
  1.3 0.7 copy-start.4
  1.3 0.7 copy-start.5
  1.3 0.7 copy-start.6
  1.4 0.7 copy-start
  1.4 0.7 copy-start.1
  1.4 0.7 copy-start.2

commit v4 on v3

--- a/solution.py
+++ b/solution.py
@@ -17,7 +17,7 @@
 NN = ((1,), (0,))
 NT = ((1,), (1,))
 TN = ((0,), (0,))
-QKV, OUT, IN, BACK = range(4)
+QKV, OUT, IN, BACK, LATE = range(5)
 CHUNK = 32
 
 
@@ -53,9 +53,9 @@
          wq, wo, wi, wb, packs, vecs, inb, n1, cot, n2, gbr, q_s, k_s, v_s, do_s, kt_s, vt_s, att, act, gpre, gproj,
          start_s, lse_s, delta_s, resid, gres, keep, tmp1, tmp2, snd, land,
          dk_s, dv_s, gwq, gwo, gwi, gwb, yq, yo, yi, yb, zq, zo, zi, zb, fq, fi, aq, ao, ai, ab,
-         v6, v6r, vs, vy, vs2, vz, ibg, sums,
+         v6, v6r, vs, vz, ibg, sums,
          loc, pk_cs, pk_cr, pk_zs, pk_zr, wc_s, wc_r, wz_s, wz_r, wy_s, wy_r, ag_s, ag_r, rs_s, rs_r,
-         gy_s, gy_r, gz_s, gz_r, gc_s, gc_r, gf_s, gf_r, vc_s, vc_r, vy_s, vy_r, vz_s, vz_r, out_s):
+         gy_s, gy_r, gz_s, gz_r, gc_s, gc_r, gf_s, gf_r, vc_s, vc_r, vz_s, vz_r, out_s):
     n, nf, t_rows, width, rows, brows, ffc = dims
     half_w, half_f = width // 2, ffc // 2
     hc = width // n
@@ -115,6 +115,7 @@
     packs[c, f] = pack[...]
     barrier = pltpu.get_barrier_semaphore()
     peers = [on_ctx(d) for d in (1, 2, 3)] + [on_z((f + s) % nf) for s in range(1, nf)] + [on_y]
+    peers += [(c, (f + s) % nf, 1 - r) for s in range(1, nf)]
     for dev in peers:
         pl.semaphore_signal(barrier, inc=1, device_id=dev, device_id_type=MESH)
     pl.semaphore_wait(barrier, len(peers))
@@ -298,7 +299,6 @@
     w_own(IN, 0)
     w_own(IN, 1)
     w_relay(BACK, 0)
-    w_own(BACK, 1)
     for s in (3, 2):
         w_step(QKV, 0, s)
         w_step(QKV, 1, s)
@@ -328,38 +328,40 @@
     key_row = lax.broadcasted_iota(jnp.int32, (t_rows, t_rows), 0)
     query_col = lax.broadcasted_iota(jnp.int32, (t_rows, t_rows), 1)
 
-    def scores(h, qb, kb, diagonal):
-        s = dot(k_s[h, kb], q_s[h, qb], NT)
+    def allowed(qb, kb, diagonal):
         ok = key_row >= start_s[qb] - kb * t_rows
-        if diagonal:
-            ok = ok & (key_row <= query_col)
-        return jnp.where(ok, s, MASKED)
-
-    def attend(h, qb):
+        return ok & (key_row <= query_col) if diagonal else ok
+
+    def scores(h, qb, kb, ok):
+        return jnp.where(ok, dot(k_s[h, kb], q_s[h, qb], NT), MASKED)
+
+    def attend(heads, qb):
         def step(kb, carry, diagonal=False):
-            m, l, acc = carry
-            s = scores(h, qb, kb, diagonal)
-            m2 = jnp.maximum(m, jnp.max(s, 0, keepdims=True))
-            p = jnp.exp(s - m2)
-            a = jnp.exp(m - m2)
-            return m2, l * a + jnp.sum(p, 0, keepdims=True), acc * a + dot(vt_s[h, kb], p.astype(BF16), NN)
+            ok = allowed(qb, kb, diagonal)
+            out = []
+            for h, (m, l, acc) in zip(heads, carry):
+                s = scores(h, qb, kb, ok)
+                m2 = jnp.maximum(m, jnp.max(s, 0, keepdims=True))
+                p = jnp.exp(s - m2)
+                a = jnp.exp(m - m2)
+                out.append((m2, l * a + jnp.sum(p, 0, keepdims=True), acc * a + dot(vt_s[h, kb], p.astype(BF16), NN)))
+            return tuple(out)
         zero = jnp.zeros((1, t_rows), F32)
-        carry = lax.fori_loop(0, qb, step, (zero + MASKED, zero, jnp.zeros((HD, t_rows), F32)))
-        m, l, acc = step(qb, carry, True)
-        att[qb, h] = (acc / l).astype(BF16)
-        lse_s[h, qb] = m + jnp.log(l)
-
-    polls = [[(IN, 0, 1), (IN, 0, 3)], [(BACK, 0, 3), (BACK, 0, 2)], [(IN, 1, 1), (IN, 1, 3)], [], [(BACK, 1, 1)], [(BACK, 1, 3)],
-             [(IN, 0, 2)], [(IN, 1, 2)]]
+        carry = lax.fori_loop(0, qb, step, tuple((zero + MASKED, zero, jnp.zeros((HD, t_rows), F32)) for _ in heads))
+        for h, (m, l, acc) in zip(heads, step(qb, carry, True)):
+            att[qb, h] = (acc / l).astype(BF16)
+            lse_s[h, qb] = m + jnp.log(l)
+
+    polls = [[(IN, 0, 1), (BACK, 0, 3)], [(IN, 1, 1)], [(IN, 0, 3), (BACK, 0, 2)], [(IN, 1, 3)], [(IN, 0, 2)], [(IN, 1, 2)],
+             [(BACK, 1, 1)], [(BACK, 1, 3)]]
     for d in (3, 2, 1, 0):
         qb = rel(d)
         for k in range(2):
-            def heads(h, _):
-                attend(h, qb)
-                return 0
-            lax.fori_loop(k * (H // n // 2), (k + 1) * (H // n // 2), heads, 0)
+            attend((2 * k, 2 * k + 1), qb)
             for poll in polls[2 * (3 - d) + k]:
                 w_step(*poll)
+            if d == 3 and k == 1:
+                w_own(BACK, 1)
         if d == 3:
             w_arrived(OUT)
         if d == 2:
@@ -378,11 +380,7 @@
     ag_start(2, n2)
     w_step(BACK, 1, 2)
     w_arrived(IN)
-    ag_wait(1, cot, 1)
-    ag_wait(1, cot, 3)
-    w_arrived(BACK)
-
-    ibg[...] = jnp.zeros_like(ibg)
+
     for d in (0, 1, 3, 2):
         b = rel(d)
         if d == 1:
@@ -393,91 +391,123 @@
 
         def up(j, _):
             tmp1[...] = dot(n2[b], wi[j].reshape(width, half_f), NN)
-            wide = jnp.concatenate([wb[h, pl.ds(j * (nf // 2), nf // 2)].reshape(half_f, half_w) for h in range(2)], 1)
-            tmp2[...] = dot(cot[b], wide, NT)
-            bias = inb[0:1, pl.ds(pl.multiple_of(j * half_f, half_f), half_f)]
             cols = pl.ds(pl.multiple_of(j * half_f, half_f), half_f)
-
-            def one(rw, acc):
+            bias = inb[0:1, cols]
+
+            def one(rw, _):
                 a, da = gelu_both(tmp1[rw] + bias)
                 act[b, rw, cols] = a.astype(BF16)
-                gp = (tmp2[rw] * da).astype(BF16)
-                gpre[b, rw, cols] = gp
-                return acc + fold(gp.astype(F32))
-            ibg[j] += chunks(one, jnp.zeros((8, half_f), F32))
+                gpre[b, rw, cols] = da.astype(BF16)
+                return 0
+            chunks(one)
             return 0
         lax.fori_loop(0, 2, up, 0)
-        if d == 3:
-            rs_sent(0)
-        for h in range(2):
-            wide = jnp.concatenate([wi[j, pl.ds(h * (n // 2), n // 2)].reshape(half_w, half_f) for j in range(2)], 1)
-            rs_put(1, d, h, dot(gpre[b], wide, NT))
-
-    grads = {QKV: (gwq, yq, zq), OUT: (gwo, yo, zo), IN: (gwi, yi, zi), BACK: (gwb, yb, zb)}
-    alls = {QKV: aq, OUT: ao, IN: ai, BACK: ab}
+    rs_sent(0)
+    ag_wait(1, cot, 1)
+    ag_wait(1, cot, 3)
+
+    grads = {OUT: (gwo, yo, zo), IN: (gwi, yi, zi), BACK: (gwb, yb, zb)}
+    alls = {QKV: aq.at[0], LATE: aq.at[1], OUT: ao, IN: ai, BACK: ab}
+    nh = n // 2
+
+    def g_part(kind, r2, f2):
+        if kind in (QKV, LATE):
+            return gwq.at[kind // LATE, pl.ds(r2 * nh, nh), f2]
+        return block(grads[kind][0], kind, r2, f2)
+
+    def y_part(kind, f2):
+        if kind in (QKV, LATE):
+            return yq.at[kind // LATE, :, f2]
+        return grads[kind][1].at[:, f2] if kind == IN else grads[kind][1].at[f2]
+
+    def z_part(kind, f2):
+        return zq.at[kind // LATE, f2] if kind in (QKV, LATE) else grads[kind][2].at[f2]
 
     def g_y(kind):
-        g, y, _z = grads[kind]
-        send(g.at[1 - r], y, gy_s.at[kind], gy_r.at[kind], on_y)
-
-    def g_z(kind):
-        g, y, z = grads[kind]
-        arrived(y, gy_r.at[kind], on_y)
-
-        def add(i, _):
-            g[r, i] = (g[r, i].astype(F32) + y[i].astype(F32)).astype(BF16)
-            return 0
-        lax.fori_loop(0, y.shape[0], add, 0)
+        for s in (*range(1, nf), 0):
+            f2 = (f + s) % nf
+            send(g_part(kind, 1 - r, f2), y_part(kind, f2), gy_s.at[kind, f2], gy_r.at[kind, f2], on_y)
+
+    def g_z(kind, s):
+        f2 = (f + s) % nf
+        g, y = g_part(kind, r, f2), y_part(kind, f2)
+        arrived(y, gy_r.at[kind, f2], on_y)
+        if kind in (OUT, BACK):
+            g[...] = (g[...].astype(F32) + y[...].astype(F32)).astype(BF16)
+        else:
+            for i in range(y.shape[0]):
+                g[i] = (g[i].astype(F32) + y[i].astype(F32)).astype(BF16)
+        if s:
+            send(g, z_part(kind, f), gz_s.at[kind, s], gz_r.at[kind, f], on_z(f2))
+
+    def g_rest(kind, s0):
+        for s in (*range(s0, nf), 0):
+            g_z(kind, s)
+
+    def g_f(kind):
         for s in range(1, nf):
             f2 = (f + s) % nf
-            send(block(g, kind, r, f2), z.at[f], gz_s.at[kind, s], gz_r.at[kind, f], on_z(f2))
-
-    def g_f(kind):
-        g, _y, z = grads[kind]
-        for s in range(1, nf):
-            f2 = (f + s) % nf
-            arrived(z.at[f2], gz_r.at[kind, f2], on_z(f2))
-        if kind in (QKV, IN):
-            fin, k = (fq, 0) if kind == QKV else (fi, 1)
-
-            def add(i, _):
-                tot = g[r, i, f].astype(F32)
-                for s in range(1, nf):
-                    tot = tot + z[(f + s) % nf, i].astype(F32)
-                fin[i] = tot.astype(BF16)
-                return 0
-            lax.fori_loop(0, n, add, 0)
-            for d in (2, 3, 1):
-                send(fin.at[rel(d)], alls[kind].at[r, c], gc_s.at[k, d], gc_r.at[k, c], on_ctx(d))
-            alls[kind][r, c] = fin[c]
-        else:
-            tot = g[r, f].astype(F32)
-            for s in range(1, nf):
-                tot = tot + z[(f + s) % nf].astype(F32)
+            arrived(z_part(kind, f2), gz_r.at[kind, f2], on_z(f2))
+        g = g_part(kind, r, f)
+        zs = [z_part(kind, (f + s) % nf) for s in range(1, nf)]
+        if kind in (OUT, BACK):
+            tot = g[...].astype(F32)
+            for z in zs:
+                tot = tot + z[...].astype(F32)
             alls[kind][r] = tot.astype(BF16)
             send(alls[kind].at[r], alls[kind].at[r], gf_s.at[kind], gf_r.at[kind], on_y)
+            return
+        fin = fi if kind == IN else fq.at[kind // LATE]
+        for i in range(fin.shape[0]):
+            tot = g[i].astype(F32)
+            for z in zs:
+                tot = tot + z[i].astype(F32)
+            fin[i] = tot.astype(BF16)
+        if kind == IN:
+            for d in (2, 3, 1):
+                send(fin.at[rel(d)], ai.at[r, c], gc_s.at[kind, d], gc_r.at[kind, c], on_ctx(d))
+            ai[r, c] = fin[c]
+            return
+        for i in range(nh):
+            owner = r * nh + i
+            send(fin.at[i], alls[kind].at[c], gc_s.at[kind, i], gc_r.at[kind, c], (owner, f, r), owner != c)
+
+            @pl.when(owner == c)
+            def _():
+                alls[kind][c] = fin[i]
 
     def g_e(kind):
-        k = 0 if kind == QKV else 1
         a = alls[kind]
-        for d in (1, 2, 3):
-            arrived(a.at[r, rel(d)], gc_r.at[k, rel(d)], on_ctx(d))
-        send(a.at[r], a.at[r], gf_s.at[kind], gf_r.at[kind], on_y)
-
-    outs = {QKV: gq_o, OUT: go_o, IN: gi_o, BACK: gb_o}
+        if kind == IN:
+            for d in (1, 2, 3):
+                arrived(a.at[r, rel(d)], gc_r.at[kind, rel(d)], on_ctx(d))
+            send(a.at[r], a.at[r], gf_s.at[kind], gf_r.at[kind], on_y)
+            return
+
+        @pl.when(c // nh == r)
+        def _():
+            for d in (1, 2, 3):
+                arrived(a.at[rel(d)], gc_r.at[kind, rel(d)], on_ctx(d))
+        send(a, a, gf_s.at[kind], gf_r.at[kind], on_y, c // nh == r)
 
     def g_out(kind):
-        a, o = alls[kind], outs[kind]
+        a = alls[kind]
+        if kind in (QKV, LATE):
+            @pl.when(c // nh != r)
+            def _():
+                arrived(a, gf_r.at[kind], on_y)
+            h = kind // LATE
+            for c2 in range(n):
+                for j in range(3):
+                    local(a.at[c2, :, pl.ds(j * pw, pw)], gq_o.at[:, pl.ds(j * width + c2 * hc + h * pw, pw)], out_s.at[kind])
+            return
         arrived(a.at[1 - r], gf_r.at[kind], on_y)
         for h in range(2):
-            if kind in (OUT, BACK):
-                local(a.at[h], o.at[:, pl.ds(h * half_w, half_w)], out_s.at[kind])
-                continue
-            for c2 in range(n):
-                for j in range(3 if kind == QKV else 1):
-                    w = pw if kind == QKV else half_f
-                    lo = j * width + c2 * hc + h * pw if kind == QKV else c2 * ffc + h * half_f
-                    local(a.at[h, c2, :, pl.ds(j * w, w)], o.at[:, pl.ds(lo, w)], out_s.at[kind])
+            if kind == IN:
+                for c2 in range(n):
+                    local(a.at[h, c2], gi_o.at[:, pl.ds(c2 * ffc + h * half_f, half_f)], out_s.at[kind])
+            else:
+                local(a.at[h], (go_o if kind == OUT else gb_o).at[:, pl.ds(h * half_w, half_w)], out_s.at[kind])
 
     def whole(buf, cols):
         v = buf[:, :, cols]
@@ -506,6 +536,31 @@
     grad_back(1 - r)
     g_y(BACK)
     grad_back(r)
+    w_arrived(BACK)
+
+    ibg[...] = jnp.zeros_like(ibg)
+    for d in (3, 2, 1, 0):
+        b = rel(d)
+
+        def slope(j, _):
+            wide = jnp.concatenate([wb[h, pl.ds(j * (nf // 2), nf // 2)].reshape(half_f, half_w) for h in range(2)], 1)
+            tmp2[...] = dot(cot[b], wide, NT)
+            cols = pl.ds(pl.multiple_of(j * half_f, half_f), half_f)
+
+            def one(rw, acc):
+                gp = (tmp2[rw] * gpre[b, rw, cols].astype(F32)).astype(BF16)
+                gpre[b, rw, cols] = gp
+                return acc + fold(gp.astype(F32))
+            ibg[j] += chunks(one, jnp.zeros((8, half_f), F32))
+            return 0
+        lax.fori_loop(0, 2, slope, 0)
+        for h in range(2):
+            wide = jnp.concatenate([wi[j, pl.ds(h * (n // 2), n // 2)].reshape(half_w, half_f) for j in range(2)], 1)
+            rs_put(1, d, h, dot(gpre[b], wide, NT))
+    grad_in(1 - r)
+    g_y(IN)
+    g_z(BACK, 1)
+    grad_in(r)
     rs_arrived(1)
 
     def ln2_back(rw, accs):
@@ -523,19 +578,19 @@
     for i, a in zip((3, 4, 5, 2), accs):
         sums[i] = a
     ag_start(3, gbr)
-    grad_in(1 - r)
-    g_y(IN)
-    grad_in(r)
-    g_z(BACK)
-    ag_forward(3, gbr)
+    if nf > 2:
+        g_z(BACK, 2)
 
     for d in (3, 2, 1, 0):
         for h in range(2):
             rs_put(2, d, h, dot(act[rel(d)], wb[h].reshape(ffc, half_w), NN))
     ag_wait(3, gbr, 1)
-    ag_wait(3, gbr, 3)
-
-    def g_attended(b, _):
+
+    def near(t):
+        return rel(t ^ (t // 2))
+
+    def g_attended(t, _):
+        b = near(t)
         wide = jnp.concatenate([wo[h].reshape(hc, half_w) for h in range(2)], 1)
         g = dot(gbr[b], wide, NT).astype(BF16)
         gt = g.T.astype(F32).reshape(H // n, HD, t_rows)
@@ -543,8 +598,7 @@
             do_s[h, b] = g[:, h * HD:(h + 1) * HD]
             delta_s[h, b] = jnp.sum(gt[h] * att[b, h].astype(F32), 0, keepdims=True)
         return 0
-    lax.fori_loop(0, n, g_attended, 0)
-    g_z(IN)
+    lax.fori_loop(0, 2, g_attended, 0)
 
     def grad_out(h):
         tot = jnp.zeros((hc, half_w), F32)
@@ -552,45 +606,43 @@
         for b in range(n):
             tot = tot + dot(att[b].reshape(hc, t_rows), gbr[b, :, cols], NN)
         gwo[h] = tot.astype(BF16).reshape(nf, rows, half_w)
-    grad_out(1 - r)
-    g_y(OUT)
-    grad_out(r)
-
-    rs_arrived(2)
 
     def finish_out(rw, _):
         out_o[rw] = (resid[rw] + rs_rows(2, rw) + vec(7)).astype(BF16)
         return 0
-    chunks(finish_out)
-
-    def attend_back(h, e, p, qb):
-        q, do = q_s[h, qb], do_s[h, qb]
-        lse, delta = lse_s[h, qb], delta_s[h, qb]
-
-        def step(kb, dqt, diagonal=False):
-            pr = jnp.exp(scores(h, qb, kb, diagonal) - lse)
-            dp = dot(v_s[h, kb], do, NT)
-            ds = (pr * (dp - delta)).astype(BF16)
-            dv_s[kb] += dot(pr.astype(BF16), do, NN)
-            dk_s[kb] += dot(ds, q, NN)
-            return dqt + dot(kt_s[h, kb], ds, NN)
-        dqt = lax.fori_loop(0, qb, step, jnp.zeros((HD, t_rows), F32))
-        dqt = step(qb, dqt, True) * (HD ** -0.5)
-        gproj[p, qb, :, e * HD:(e + 1) * HD] = dqt.T.astype(BF16)
-
-    def pair_back(p):
+
+    def pair_blocks(p, lo, hi):
+        def one(t, _):
+            qb = near(t)
+
+            def step(kb, dqts, diagonal=False):
+                ok = allowed(qb, kb, diagonal)
+                out = []
+                for e in range(2):
+                    h = 2 * p + e
+                    q, do = q_s[h, qb], do_s[h, qb]
+                    pr = jnp.exp(scores(h, qb, kb, ok) - lse_s[h, qb])
+                    dp = dot(v_s[h, kb], do, NT)
+                    ds = (pr * (dp - delta_s[h, qb])).astype(BF16)
+                    dv_s[e, kb] += dot(pr.astype(BF16), do, NN)
+                    dk_s[e, kb] += dot(ds, q, NN)
+                    out.append(dqts[e] + dot(kt_s[h, kb], ds, NN))
+                return tuple(out)
+            dqts = lax.fori_loop(0, qb, step, (jnp.zeros((HD, t_rows), F32),) * 2)
+            for e, dqt in enumerate(step(qb, dqts, True)):
+                gproj[p, qb, :, e * HD:(e + 1) * HD] = (dqt * (HD ** -0.5)).T.astype(BF16)
+            return 0
+        lax.fori_loop(lo, hi, one, 0)
+
+    def pair_start():
+        dk_s[...] = jnp.zeros_like(dk_s)
+        dv_s[...] = jnp.zeros_like(dv_s)
+
+    def pair_end(p):
         for e in range(2):
-            h = 2 * p + e
-            dk_s[...] = jnp.zeros_like(dk_s)
-            dv_s[...] = jnp.zeros_like(dv_s)
-
-            def one(qb, _):
-                attend_back(h, e, p, qb)
-                return 0
-            lax.fori_loop(0, n, one, 0)
             for b in range(n):
-                gproj[p, b, :, pw + e * HD:pw + (e + 1) * HD] = dk_s[b].astype(BF16)
-                gproj[p, b, :, 2 * pw + e * HD:2 * pw + (e + 1) * HD] = dv_s[b].astype(BF16)
+                gproj[p, b, :, pw + e * HD:pw + (e + 1) * HD] = dk_s[e, b].astype(BF16)
+                gproj[p, b, :, 2 * pw + e * HD:2 * pw + (e + 1) * HD] = dv_s[e, b].astype(BF16)
 
         def grad_qkv(i, _):
             a = whole(n1, pl.ds(pl.multiple_of(i * hc, hc), hc))
@@ -598,20 +650,45 @@
             return 0
         lax.fori_loop(0, n, grad_qkv, 0)
 
-    pair_back(1 - r)
+    pair_start()
+    pair_blocks(0, 0, 2)
+    g_rest(BACK, 3)
+    ag_forward(3, gbr)
+    ag_wait(3, gbr, 3)
+    lax.fori_loop(2, n, g_attended, 0)
+    pair_blocks(0, 2, n)
+    g_z(IN, 1)
+    pair_end(0)
     g_y(QKV)
-    g_f(BACK)
-    g_z(OUT)
-    pair_back(r)
+    grad_out(1 - r)
+    g_y(OUT)
+    grad_out(r)
+    rs_arrived(2)
+    chunks(finish_out)
+    if nf > 2:
+        g_z(IN, 2)
+    pair_start()
+    pair_blocks(1, 0, 2)
+    g_rest(IN, 3)
+    pair_blocks(1, 2, n)
+    g_z(QKV, 1)
+    if nf > 2:
+        g_z(QKV, 2)
+    pair_end(1)
+    g_y(LATE)
+    g_rest(QKV, 3)
     rs_sent(1)
     for d in (3, 2, 1, 0):
         for h in range(2):
             gp = jnp.concatenate([gproj[p, rel(d)] for p in range(2)], 1)
             wide = jnp.concatenate([wq[p, pl.ds(h * (n // 2), n // 2)].reshape(half_w, 3 * pw) for p in range(2)], 1)
             rs_put(3, d, h, dot(gp, wide, NT))
-    g_z(QKV)
     g_f(IN)
-    g_f(OUT)
+    g_f(BACK)
+    g_rest(OUT, 1)
+    g_rest(LATE, 1)
+    g_f(QKV)
+    g_e(IN)
     rs_arrived(3)
 
     def ln1_back(rw, accs):
@@ -623,6 +700,8 @@
     accs = chunks(ln1_back, (zero8, zero8), 16)
     sums[0], sums[1] = accs[0], accs[1]
 
+    g_e(QKV)
+    g_f(OUT)
     for i in range(8):
         row = jnp.sum(sums[i], 0, keepdims=True) if i < 6 else jnp.zeros((1, width), F32)
         for c2 in range(n):
@@ -642,22 +721,21 @@
     for d in (1, 2, 3):
         arrived(v6r.at[rel(d)], vc_r.at[rel(d)], on_ctx(d))
     vs[0:8] = v6[c] + v6r[rel(1)] + v6r[rel(2)] + v6r[rel(3)]
-    send(vs, vy, vy_s.at[0], vy_r.at[0], on_y)
-    g_e(IN)
-    g_f(QKV)
-    arrived(vy, vy_r.at[0], on_y)
-    vs2[...] = vs[...] + vy[...]
-    for s in range(1, nf):
-        send(vs2, vz.at[f], vz_s.at[s], vz_r.at[f], on_z((f + s) % nf))
-    g_e(QKV)
+    me = r * nf + f
+    vz[me] = vs[...]
+    for k in range(1, 2 * nf):
+        f2, r2 = (f + k) % nf, (r + k // nf) % 2
+        send(vs, vz.at[me], vz_s.at[k], vz_r.at[me], (c, f2, r2))
+    g_f(LATE)
+    g_e(LATE)
     g_out(BACK)
     g_out(OUT)
-    g_out(IN)
-    tot = vs2[...]
-    for s in range(1, nf):
-        f2 = (f + s) % nf
-        arrived(vz.at[f2], vz_r.at[f2], on_z(f2))
-        tot = tot + vz[f2]
+    for k in range(1, 2 * nf):
+        f2, r2 = (f + k) % nf, (r + k // nf) % 2
+        arrived(vz.at[r2 * nf + f2], vz_r.at[r2 * nf + f2], (c, f2, r2))
+    tot = vz[0]
+    for k in range(1, 2 * nf):
+        tot = tot + vz[k]
     mine, mine_in = tot[:, :rows], tot[8:9, :4 * rows]
     for f2 in range(1, nf):
         row, lo = 8 + f2 * 4 * rows // hc, f2 * 4 * rows % hc
@@ -665,12 +743,14 @@
         mine_in = jnp.where(f == f2, tot[row:row + 1, lo:lo + 4 * rows], mine_in)
     gv_o[0:16, :rows] = mine
     gv_o[16:17, :4 * rows] = mine_in
+    g_out(IN)
     g_out(QKV)
+    g_out(LATE)
     rs_sent(2)
     rs_sent(3)
     for end in ends:
         end()
-    for kind in range(4):
+    for kind in range(5):
         local_done(alls[kind], out_s.at[kind])
 
 
@@ -715,18 +795,18 @@
         vm((n, 1, t_rows), jnp.int32), vm((heads, n, 1, t_rows), F32), vm((heads, n, 1, t_rows), F32),
         vm((t_rows, width), F32), vm((t_rows, width), F32), vm((t_rows, width), F32), vm((t_rows, half_f), F32), vm((t_rows, half_f), F32),
         vm((2, 3, 2, t_rows, half_w), BF16), vm((4, 3, 2, t_rows, half_w), BF16),
-        vm((n, t_rows, HD), F32), vm((n, t_rows, HD), F32),
+        vm((2, n, t_rows, HD), F32), vm((2, n, t_rows, HD), F32),
         vm((2, n, nf, rows, q3), BF16), vm((2, nf, rows, half_w), BF16), vm((2, n, nf, rows, half_f), BF16), vm((2, nf, brows, half_w), BF16),
-        vm((n, nf, rows, q3), BF16), vm((nf, rows, half_w), BF16), vm((n, nf, rows, half_f), BF16), vm((nf, brows, half_w), BF16),
-        vm((nf, n, rows, q3), BF16), vm((nf, rows, half_w), BF16), vm((nf, n, rows, half_f), BF16), vm((nf, brows, half_w), BF16),
-        vm((n, rows, q3), BF16), vm((n, rows, half_f), BF16),
+        vm((2, n // 2, nf, rows, q3), BF16), vm((nf, rows, half_w), BF16), vm((n, nf, rows, half_f), BF16), vm((nf, brows, half_w), BF16),
+        vm((2, nf, n // 2, rows, q3), BF16), vm((nf, rows, half_w), BF16), vm((nf, n, rows, half_f), BF16), vm((nf, brows, half_w), BF16),
+        vm((2, n // 2, rows, q3), BF16), vm((n, rows, half_f), BF16),
         vm((2, n, rows, q3), BF16), vm((2, rows, half_w), BF16), vm((2, n, rows, half_f), BF16), vm((2, brows, half_w), BF16),
-        vm((n, 8, hc), F32), vm((n, 8, hc), F32), vm((16, hc), F32), vm((16, hc), F32), vm((16, hc), F32), vm((nf, 16, hc), F32),
+        vm((n, 8, hc), F32), vm((n, 8, hc), F32), vm((16, hc), F32), vm((2 * nf, 16, hc), F32),
         vm((2, 8, half_f), F32), vm((8, 8, width), F32),
         dma((5,)), dma((4,)), dma((n,)), dma((nf,)), dma((nf,)), dma((2, 4)), dma((2, n)),
         dma((4, 2, 4 + 2 * max(0, nf - 3))), dma((4, 2, nf)), dma((4, 2, nf)), dma((4, 2, nf)), dma((4, 3)), dma((4, n)), dma((4, 3, 2)), dma((4, 3, 2)),
-        dma((4,)), dma((4,)), dma((4, nf)), dma((4, nf)), dma((2, 4)), dma((2, n)), dma((4,)), dma((4,)),
-        dma((4,)), dma((n,)), dma((1,)), dma((1,)), dma((nf,)), dma((nf,)), dma((4,)),
+        dma((5, nf)), dma((5, nf)), dma((5, nf)), dma((5, nf)), dma((5, 4)), dma((5, n)), dma((5,)), dma((5,)),
+        dma((4,)), dma((n,)), dma((2 * nf,)), dma((2 * nf,)), dma((5,)),
     ]
     shape = jax.ShapeDtypeStruct
     in_vmem, in_hbm = pl.BlockSpec(memory_space=vm), pl.BlockSpec(memory_space=pl.ANY)

time: 213 us -> 203 us (0.953)
  Pallas kernels: 204 us -> 195 us
    pallas_call x1, Pallas kernels: 201 us -> 192 us  [shards(): pl.pallas_call(functools.partial(body, dims), out_shape=[shape((t_rows, w...]
where the time goes in v4:
time: 203 us; the launch traced here: 201 us
  Pallas kernels  195 us (96%)
  local copies, waits for them, and re-layouts  4.84 us (2%)
    pallas_call x1, Pallas kernels, shards(): pl.pallas_call(functools.partial(body, dims), out_shape=[shape((t_rows, w...  192 us

profile of v4, /device:TPU:29, one launch (start us, length us, event | category | flops | bytes accessed | tf_op | source)
XLA Modules:
  0.0 200.9 jit_solution(18105662918918809413)
XLA Ops:
  0.6 0.0 copy-start.8
  0.7 0.0 copy-start.7
  0.7 0.6 copy-done.8
  1.3 0.0 copy-start.3
  1.3 0.0 copy-start.4
  1.3 0.0 copy-start.5
  1.3 0.0 copy-start.6
  1.3 0.1 reshape.33
  1.4 0.0 copy-start
  1.4 0.0 copy-start.1
  1.4 0.0 copy-start.2
  1.4 0.0 copy-done.7
  1.4 0.5 copy-done.3
  2.0 0.0 copy-done.4
  2.0 0.0 copy-done.5
  2.0 0.0 copy-done.6
  2.0 0.0 copy-done
  2.1 0.0 copy-done.1
  2.1 0.0 copy-done.2
  2.1 0.1 concatenate.3
  2.1 0.6 pad.4.pack
  2.8 191.8 %shard_map.271 = (bf16[256,1024]{1,0:T(8,128)(2,1)}, f32[256,1024]{1,0:T(8,128)}, bf16[64,3072]{1,0:T(8,128)(2,1)}, bf16[64,1024]{1,0:T(8,128)(2,1)}, bf16[64,40...) custom-call(bf16[256,1024]{1,0:T(8,128)(2,1)} %bitcast.29, bf16[256,1024]{1,0:T(8,128)(2,1)} %bitcast.30, ...), custom_call_target="tpu_custom_call" | custom-call | tf_op jit(solution)/shard_map/pallas_call | solution.py:813
  194.6 1.3 slice.43
  195.9 1.5 slice_bitcast_fusion
  197.4 3.4 %shard_map.272 = (bf16[256,1024]{1,0:T(8,128)(2,1)}, f32[256,1024]{1,0:T(8,128)}, f32[64,3072]{1,0:T(8,128)}, f32[64,1024]{1,0:T(8,128)}, f32[64,4096]{1,0:T(8,128)}, /*index=5*/f32[256,1024]{1,0:T(8,128)}) custom-call(bf16[256,1024]{1,0:T(8,128)(2,1)} %get-tuple-element.28.lo_i, f32[256,1024]{1,0:T(8,128)} %get-tuple-element.29.gx_i, ...), custom_call_target="tpu_custom_call" | custom-call | tf_op jit(solution)/shard_map/pallas_call | solution.py:824
  (1 shorter events, 0.0 us)
Async XLA Ops:
  0.6 0.7 copy-start.8
  0.7 0.8 copy-start.7
  1.3 0.7 copy-start.3
  1.3 0.7 copy-start.4
  1.3 0.7 copy-start.5
  1.3 0.7 copy-start.6
  1.4 0.7 copy-start
  1.4 0.7 copy-start.1
  1.4 0.7 copy-start.2

commit v5 on v4

--- a/solution.py
+++ b/solution.py
@@ -655,25 +655,28 @@
     g_rest(BACK, 3)
     ag_forward(3, gbr)
     ag_wait(3, gbr, 3)
+    g_z(IN, 1)
     lax.fori_loop(2, n, g_attended, 0)
-    pair_blocks(0, 2, n)
-    g_z(IN, 1)
+    pair_blocks(0, 2, 3)
+    if nf > 2:
+        g_z(IN, 2)
+    pair_blocks(0, 3, n)
+    for s in range(3, nf):
+        g_z(IN, s)
     pair_end(0)
     g_y(QKV)
+    g_z(IN, 0)
     grad_out(1 - r)
     g_y(OUT)
     grad_out(r)
     rs_arrived(2)
     chunks(finish_out)
-    if nf > 2:
-        g_z(IN, 2)
     pair_start()
     pair_blocks(1, 0, 2)
-    g_rest(IN, 3)
-    pair_blocks(1, 2, n)
     g_z(QKV, 1)
     if nf > 2:
         g_z(QKV, 2)
+    pair_blocks(1, 2, n)
     pair_end(1)
     g_y(LATE)
     g_rest(QKV, 3)

time: 203 us -> 198 us (0.975)
  Pallas kernels: 195 us -> 192 us
    pallas_call x1, Pallas kernels: 192 us -> 189 us  [shards(): pl.pallas_call(functools.partial(body, dims), out_shape=[shape((t_rows, w...]
where the time goes in v5:
time: 198 us
  Pallas kernels  192 us (97%)
  local copies, waits for them, and re-layouts  4.84 us (2%)
    pallas_call x1, Pallas kernels, shards(): pl.pallas_call(functools.partial(body, dims), out_shape=[shape((t_rows, w...  189 us

profile of v5, /device:TPU:29, one launch (start us, length us, event | category | flops | bytes accessed | tf_op | source)
XLA Modules:
  0.0 197.8 jit_solution(1441930246147552907)
XLA Ops:
  0.6 0.0 copy-start.8
  0.7 0.0 copy-start.7
  0.7 0.6 copy-done.8
  1.3 0.0 copy-start.3
  1.3 0.0 copy-start.4
  1.3 0.0 copy-start.5
  1.3 0.0 copy-start.6
  1.3 0.1 reshape.33
  1.4 0.0 copy-start
  1.4 0.0 copy-start.1
  1.4 0.0 copy-start.2
  1.4 0.0 copy-done.7
  1.4 0.5 copy-done.3
  2.0 0.0 copy-done.4
  2.0 0.0 copy-done.5
  2.0 0.0 copy-done.6
  2.0 0.0 copy-done
  2.1 0.0 copy-done.1
  2.1 0.0 copy-done.2
  2.1 0.1 concatenate.3
  2.1 0.6 pad.4.pack
  2.8 188.7 %shard_map.271 = (bf16[256,1024]{1,0:T(8,128)(2,1)}, f32[256,1024]{1,0:T(8,128)}, bf16[64,3072]{1,0:T(8,128)(2,1)}, bf16[64,1024]{1,0:T(8,128)(2,1)}, bf16[64,40...) custom-call(bf16[256,1024]{1,0:T(8,128)(2,1)} %bitcast.29, bf16[256,1024]{1,0:T(8,128)(2,1)} %bitcast.30, ...), custom_call_target="tpu_custom_call" | custom-call | tf_op jit(solution)/shard_map/pallas_call | solution.py:816
  191.4 1.3 slice.43
  192.7 1.5 slice_bitcast_fusion
  194.2 3.4 %shard_map.272 = (bf16[256,1024]{1,0:T(8,128)(2,1)}, f32[256,1024]{1,0:T(8,128)}, f32[64,3072]{1,0:T(8,128)}, f32[64,1024]{1,0:T(8,128)}, f32[64,4096]{1,0:T(8,128)}, /*index=5*/f32[256,1024]{1,0:T(8,128)}) custom-call(bf16[256,1024]{1,0:T(8,128)(2,1)} %get-tuple-element.28.lo_i, f32[256,1024]{1,0:T(8,128)} %get-tuple-element.29.gx_i, ...), custom_call_target="tpu_custom_call" | custom-call | tf_op jit(solution)/shard_map/pallas_call | solution.py:827
  (1 shorter events, 0.0 us)
Async XLA Ops:
  0.6 0.7 copy-start.8
  0.7 0.8 copy-start.7
  1.3 0.7 copy-start.3
  1.3 0.7 copy-start.4
  1.3 0.7 copy-start.5
  1.3 0.7 copy-start.6
  1.4 0.7 copy-start
  1.4 0.7 copy-start.1
  1.4 0.7 copy-start.2
